TPU v7x, 32 devices: a whole 2x2x4 slice. The times are simulated.
32 devices in a mesh: gx: 8 (over z, x), yz: 4 (over y, core).
Axes of the slice: x: 2, y: 2, z: 4, core: 2. Of those that a mesh axis runs over, the one named last changes fastest.
Arguments:
- populations: float32 [19, 64, 32, 128], P(None, 'gx', 'yz'), may hold values from 0.02 to 0.1
- cell_grain: int32 [64, 32, 128], P('gx', 'yz'), may hold values from -1 to 1023, as said below
- near_rows: int32 [32, 1024], P(('gx', 'yz')), may hold values from -1 to 511, as said below
- contact_pairs: int32 [2, 32768], P(None, ('gx', 'yz')), may hold values from 0 to 1023, as said below
- grain_position: float32 [3, 16384], P(None, ('gx', 'yz')), may hold values from 0 to 6
- grain_velocity: float32 [3, 16384], P(None, ('gx', 'yz')), may hold values from -0.1 to 0.1
- grain_radius: float32 [16384], P(('gx', 'yz')), may hold values from 0.8 to 1.6
- grain_mass: float32 [16384], P(('gx', 'yz')), may hold values from 2 to 20
Outputs:
- populations_next: float32 [19, 64, 32, 128], P(None, 'gx', 'yz')
- velocity_next: float32 [3, 16384], P(None, ('gx', 'yz'))
- position_next: float32 [3, 16384], P(None, ('gx', 'yz'))
Inputs may be any that keep to these rules, and one draw needn't show every extreme that they name: `near_rows`: entry o * 32 + s of device d's row names a row of device o's grains or is -1; in each block of 32 entries the live ones come first, are distinct, and number 1 to 32; every device has one block with all 32 live. `cell_grain`: A solid cell names a live entry of the list of the device whose brick holds it; the share of solid cells differs from brick to brick. `contact_pairs`: column p belongs to device p // 1024: its first row is a row of that device's grains, its second a live entry of that device's list.
All inputs are finite; a program needn't handle non-finite values.
Results may differ from a plain program's by a relative error of at most 0.0003.
Values sent between devices are 32-bit elements; how exact they have to be, the bound alone decides.
A program may use at most 64 MiB of HBM per device.

v0:
```python
import math

import jax
import jax.numpy as jnp
import numpy as np
from jax import lax
from jax.sharding import PartitionSpec as P

lattice_dirs = (
    (0, 0, 0),
    (1, 0, 0),
    (-1, 0, 0),
    (0, 1, 0),
    (0, -1, 0),
    (0, 0, 1),
    (0, 0, -1),
    (1, 1, 0),
    (-1, -1, 0),
    (1, -1, 0),
    (-1, 1, 0),
    (1, 0, 1),
    (-1, 0, -1),
    (1, 0, -1),
    (-1, 0, 1),
    (0, 1, 1),
    (0, -1, -1),
    (0, 1, -1),
    (0, -1, 1),
)
lattice_weights = (1.0 / 3.0,) + (1.0 / 18.0,) * 6 + (1.0 / 36.0,) * 12
opposite = (0, 2, 1, 4, 3, 6, 5, 8, 7, 10, 9, 12, 11, 14, 13, 16, 15, 18, 17)
relax_rate = 1.25
stiffness = 0.5
damping = 0.5
highest = lax.Precision.HIGHEST


def extended(block, sides, width):
    for axis, dim in sides:
        count = lax.axis_size(axis)
        forward = [(i, i + 1) for i in range(count - 1)]
        forward.append((count - 1, 0))
        backward = [(target, source) for source, target in forward]
        low = lax.ppermute(
            lax.slice_in_dim(block, block.shape[dim] - width, None, axis=dim), axis, forward
        )
        high = lax.ppermute(lax.slice_in_dim(block, 0, width, axis=dim), axis, backward)
        block = jnp.concatenate([low, block, high], axis=dim)
    return block


def project(direction, parts):
    total = None
    for compo in range(3):
        factor = lattice_dirs[direction][compo]
        if factor != 0:
            term = factor * parts[compo]
            total = term if total is None else total + term
    return total


def indicator(ids, count):
    return (ids[..., None] == jnp.arange(count, dtype=jnp.int32)).astype(jnp.float32)


def collide(populations):
    vectors = jnp.asarray(np.array(lattice_dirs, np.float32))
    weights = jnp.asarray(np.array(lattice_weights, np.float32))[:, None, None, None]
    density = jnp.sum(populations, axis=0)
    speeds = jnp.einsum("ic,ixyz->cxyz", vectors, populations, precision=highest) / density[None]
    square = jnp.sum(speeds * speeds, axis=0)
    along = jnp.einsum("ic,cxyz->ixyz", vectors, speeds, precision=highest)
    equil = weights * density[None] * (1.0 + 3.0 * along + 4.5 * along * along - 1.5 * square[None])
    return populations + relax_rate * (equil - populations)


def stream_force(populations, fluid, padded):
    width_x = populations.shape[1]
    width_y = populations.shape[2]

    def shifted(low, high, shift_x, shift_y, shift_z):
        piece = padded[
            low:high, 1 - shift_x : 1 - shift_x + width_x, 1 - shift_y : 1 - shift_y + width_y
        ]
        if shift_z != 0:
            piece = jnp.roll(piece, shift_z, axis=3)
        return piece

    here = shifted(0, 24, 0, 0, 0)
    fresh = [here[0]]
    force = [jnp.zeros_like(here[0]) for compo in range(3)]
    for direction in range(1, 19):
        shift_x, shift_y, shift_z = lattice_dirs[direction]
        back = opposite[direction]
        weight = lattice_weights[direction]
        source_pop = shifted(direction, direction + 1, shift_x, shift_y, shift_z)[0]
        source_aux = shifted(19, 23, shift_x, shift_y, shift_z)
        bounce = here[back] + 6.0 * weight * here[23] * project(direction, source_aux[0:3])
        fresh.append(source_aux[3] * source_pop + (1.0 - source_aux[3]) * bounce)
        target_pop = shifted(back, back + 1, -shift_x, -shift_y, -shift_z)[0]
        target_aux = shifted(22, 24, -shift_x, -shift_y, -shift_z)
        link = (
            target_aux[0]
            * (2.0 * target_pop + 6.0 * weight * target_aux[1] * project(direction, here[19:22]))
            * (1.0 - here[22])
        )
        for compo in range(3):
            factor = lattice_dirs[direction][compo]
            if factor != 0:
                force[compo] = force[compo] - factor * link
    read = jnp.where(fluid[None], jnp.stack(fresh), populations)
    return (read, jnp.stack(force))


def contact_force(pos_a, vel_a, rad_a, pos_b, vel_b, rad_b):
    offset = pos_a - pos_b
    length = jnp.sqrt(jnp.sum(offset * offset, axis=0))
    normal = offset / jnp.maximum(length, 1.0)
    intersection = jnp.maximum(rad_a + rad_b - length, 0.0)
    closing = jnp.sum((vel_a - vel_b) * normal, axis=0)
    return (stiffness * intersection - damping * intersection * closing) * normal


def local(
    populations,
    cell_grain,
    near_rows,
    contact_pairs,
    grain_position,
    grain_velocity,
    grain_radius,
    grain_mass,
):
    devices = lax.axis_size(("gx", "yz"))
    near_count = near_rows.shape[1]
    slot_count = near_count // devices
    owned = grain_position.shape[1]
    width_x = populations.shape[1]
    width_y = populations.shape[2]
    depth = populations.shape[3]
    plane = width_y * depth
    local_state = jnp.concatenate([grain_position, grain_velocity, grain_radius[None]], 0)
    asked = lax.all_to_all(
        near_rows.reshape(devices, slot_count),
        ("gx", "yz"),
        split_axis=0,
        concat_axis=0,
        tiled=True,
    )
    row_table = indicator(asked, owned)
    answer = jnp.einsum("cg,osg->cos", local_state, row_table, precision=highest)
    near_state = lax.all_to_all(
        answer, ("gx", "yz"), split_axis=1, concat_axis=1, tiled=True
    ).reshape(7, near_count)
    solid = cell_grain >= 0
    plane_ids = cell_grain.reshape(width_x, plane)
    near_wall = near_state[3:6]

    def wall_plane(ids):
        return jnp.einsum("cn,kn->ck", near_wall, indicator(ids, near_count), precision=highest)

    wall = jnp.moveaxis(lax.map(wall_plane, plane_ids), 1, 0).reshape(3, width_x, width_y, depth)
    post = collide(populations)
    table = jnp.concatenate([post, wall, (~solid).astype(jnp.float32)[None]], 0)
    padded = extended(table, (("gx", 1), ("yz", 2)), 1)
    padded = jnp.concatenate([padded, jnp.sum(padded[:19], axis=0)[None]], 0)
    read, cell_force = stream_force(populations, ~solid, padded)
    force_planes = jnp.moveaxis(cell_force.reshape(3, width_x, plane), 1, 0)

    def add_plane(total, inputs):
        ids, forces = inputs
        return (
            total + jnp.einsum("ck,kn->cn", forces, indicator(ids, near_count), precision=highest),
            None,
        )

    slot_force, unused = lax.scan(
        add_plane, jnp.zeros((3, near_count), jnp.float32), (plane_ids, force_planes)
    )
    returned = lax.all_to_all(
        slot_force.reshape(3, devices, slot_count),
        ("gx", "yz"),
        split_axis=1,
        concat_axis=1,
        tiled=True,
    )
    fluid_force = jnp.einsum("cos,osg->cg", returned, row_table, precision=highest)
    pair_count = contact_pairs.shape[1]
    block = math.gcd(pair_count, 1024)
    first_blocks = contact_pairs[0].reshape(pair_count // block, block)
    second_blocks = contact_pairs[1].reshape(pair_count // block, block)

    def add_pairs(total, inputs):
        first, second = inputs
        first_table = indicator(first, owned)
        second_table = indicator(second, near_count)
        state_a = jnp.einsum("cg,pg->cp", local_state, first_table, precision=highest)
        state_b = jnp.einsum("cn,pn->cp", near_state, second_table, precision=highest)
        push = contact_force(
            state_a[0:3], state_a[3:6], state_a[6], state_b[0:3], state_b[3:6], state_b[6]
        )
        return (total + jnp.einsum("cp,pg->cg", push, first_table, precision=highest), None)

    contact_total, unused = lax.scan(
        add_pairs, jnp.zeros((3, owned), jnp.float32), (first_blocks, second_blocks)
    )
    velocity_next = grain_velocity + (fluid_force + contact_total) / grain_mass[None]
    position_next = grain_position + velocity_next
    return (read, velocity_next, position_next)


def solution(mesh):
    return jax.shard_map(
        local,
        mesh=mesh,
        in_specs=(
            P(None, "gx", "yz", None),
            P("gx", "yz", None),
            P(("gx", "yz"), None),
            P(None, ("gx", "yz")),
            P(None, ("gx", "yz")),
            P(None, ("gx", "yz")),
            P(("gx", "yz")),
            P(("gx", "yz")),
        ),
        out_specs=(P(None, "gx", "yz", None), P(None, ("gx", "yz")), P(None, ("gx", "yz"))),
        check_vma=False,
    )
```

profile of v0, /device:TPU:0, one launch (start us, length us, event | category | flops | bytes accessed | tf_op | source)
XLA Modules:
  0.0 113.5 jit_solution(1112594718275254140)
XLA Ops:
  0.7 0.5 broadcast.423
  1.2 1.3 %reduce.3 = s32[1024]{0:T(1024)S(1)} reduce(s32[1,1024]{1,0:T(1,128)} %param.16, s32[]{:T(128)} %broadcast.423), dimensions={0}, to_apply=%param.16.reduce_sub_computation.3 | reduce | bytes 8196 | tf_op args[2]
  2.5 0.7 all_to_all.12
  3.2 7.3 %all-to-all-start = ((s32[32,1,32]{2,1,0:T(1,128)}), s32[32,1,32]{2,1,0:T(1,128)S(1)}, u32[]{:S(2)}, u32[]{:S(2)}) async-start(s32[32,1,32]{2,1,0:T(1,128)} %all_to_all.12), calls=%async_computation | async-start | bytes 32768 | tf_op jit(solution)/shard_map/all_to_all | solution.py:143
  10.5 1.1 reduce_sum.49
  11.7 2.0 %multiply_reduce_fusion = (f32[8,8,128]{2,1,0:T(8,128)S(1)}, f32[3,8,8,128]{3,0,2,1:T(4,128)S(1)}) fusion(f32[8,8,128]{2,1,0:T(8,128)S(1)} %reduce_sum.49, f32[19,3,1,1]{0,1,3,2:T(4,128)} %constant.67, f32[19,8,8,128]{3,2,1,0:T(8,128)} %param.14), kind=kOutput, calls=%fused_computation.61 | convolution fusion | flops 5668864 | bytes 786660 | tf_op jit(solution)/shard_map/ic,ixyz->cxyz/dot_general | solution.py:70
  13.7 1.6 %fusion.282 = f32[19,8,8,128]{3,0,2,1:T(8,128)S(1)} fusion(f32[19,3,1,1]{0,1,3,2:T(4,128)} %constant.67, f32[3,8,8,128]{3,0,2,1:T(4,128)S(1)} %get-tuple-element.149), kind=kOutput, calls=%fused_computation.547 | convolution fusion | flops 5603328 | bytes 721124 | tf_op jit(solution)/shard_map/ic,cxyz->ixyz/dot_general | solution.py:72
  15.6 0.6 fusion.273
  16.2 0.7 fusion.274
  16.9 0.6 convert_bitcast_fusion
  17.7 2.2 %fusion.279 = f32[32,7,32]{2,1,0:T(8,128)S(1)} fusion(s32[32,32]{1,0:T(8,128)S(1)} %bitcast.272, f32[1,512]{1,0:T(1,128)S(1)} %bitcast.278, f32[3,512]{1,0:T(4,128)S(1)} %copy-done.24, f32[3,512]{1,0:T(4,128)S(1)} %copy-done.26), kind=kOutput, calls=%fused_computation.546 | convolution fusion | flops 44571648 | bytes 47104 | tf_op jit(solution)/shard_map/cg,osg->cos/dot_general | solution.py:151
  19.9 0.8 reshape.459
  20.6 5.7 %all-to-all-start.1 = ((f32[32,1,224]{2,1,0:T(1,128)}), f32[32,1,224]{2,1,0:T(1,128)S(1)}, u32[]{:S(2)}, u32[]{:S(2)}) async-start(f32[32,1,224]{2,1,0:T(1,128)} %reshape.459), calls=%async_computation.1 | async-start | bytes 65536 | tf_op jit(solution)/shard_map/all_to_all | solution.py:152
  26.4 1.1 fusion.13
  27.5 6.1 %all-to-all-done.1 = f32[32,1,224]{2,1,0:T(1,128)S(1)} async-done(((f32[32,1,224]{2,1,0:T(1,128)}), f32[32,1,224]{2,1,0:T(1,128)S(1)}, u32[]{:S(2)}, u32[]{:S(2)}) %all-to-all-start.1) | async-done | bytes 28704 | tf_op jit(solution)/shard_map/all_to_all | solution.py:152
  33.6 0.5 broadcast.424
  34.1 0.7 reduce.4
  35.1 16.3 %while.25 = (s32[]{:T(128)}, f32[8,3,1024]{2,1,0:T(4,128)S(1)}, s32[8,1024]{1,0:T(8,128)S(1)}, f32[3,1024]{1,0:T(4,128)S(1)}, s32[]{:T(128)}) while((s32[]{:T(128)}, f32[8,3,1024]{2,1,0:T(4,128)S(1)}, s32[8,1024]{1,0:T(8,128)S(1)}, f32[3,1024]{1,0:T(4,128)S(1)}, s32[]{:T(128)}) %tuple.81), condition=%wide.region_3.4_spmd, body=%wide.region_2.3_spmd.sunk | while | flops 38797312 | bytes 45125 | solution.py:162
  35.1 2.0 %fusion.321 = f32[8,3,1024]{2,1,0:T(4,128)S(1)} fusion(f32[8,3,1024]{2,1,0:T(4,128)S(1)} %get-tuple-element.208, s32[]{:T(128)} %get-tuple-element.207, f32[3,1024]{1,0:T(4,128)S(1)} %get-tuple-element.215, s32[1024]{0:T(1024)S(1)} %bitcast.269), kind=kOutput, calls=%fused_computation.4.clone.1 | convolution fusion | flops 38797312 | bytes 36868 | tf_op jit(solution)/shard_map/while/body/eval_jaxpr/cn,kn->ck/dot_general | solution.py:160
  37.1 2.0 %fusion.321 = f32[8,3,1024]{2,1,0:T(4,128)S(1)} fusion(f32[8,3,1024]{2,1,0:T(4,128)S(1)} %get-tuple-element.208, s32[]{:T(128)} %get-tuple-element.207, f32[3,1024]{1,0:T(4,128)S(1)} %get-tuple-element.215, s32[1024]{0:T(1024)S(1)} %bitcast.269), kind=kOutput, calls=%fused_computation.4.clone.1 | convolution fusion | flops 38797312 | bytes 36868 | tf_op jit(solution)/shard_map/while/body/eval_jaxpr/cn,kn->ck/dot_general | solution.py:160
  39.2 2.0 %fusion.321 = f32[8,3,1024]{2,1,0:T(4,128)S(1)} fusion(f32[8,3,1024]{2,1,0:T(4,128)S(1)} %get-tuple-element.208, s32[]{:T(128)} %get-tuple-element.207, f32[3,1024]{1,0:T(4,128)S(1)} %get-tuple-element.215, s32[1024]{0:T(1024)S(1)} %bitcast.269), kind=kOutput, calls=%fused_computation.4.clone.1 | convolution fusion | flops 38797312 | bytes 36868 | tf_op jit(solution)/shard_map/while/body/eval_jaxpr/cn,kn->ck/dot_general | solution.py:160
  41.2 2.0 %fusion.321 = f32[8,3,1024]{2,1,0:T(4,128)S(1)} fusion(f32[8,3,1024]{2,1,0:T(4,128)S(1)} %get-tuple-element.208, s32[]{:T(128)} %get-tuple-element.207, f32[3,1024]{1,0:T(4,128)S(1)} %get-tuple-element.215, s32[1024]{0:T(1024)S(1)} %bitcast.269), kind=kOutput, calls=%fused_computation.4.clone.1 | convolution fusion | flops 38797312 | bytes 36868 | tf_op jit(solution)/shard_map/while/body/eval_jaxpr/cn,kn->ck/dot_general | solution.py:160
  43.2 2.0 %fusion.321 = f32[8,3,1024]{2,1,0:T(4,128)S(1)} fusion(f32[8,3,1024]{2,1,0:T(4,128)S(1)} %get-tuple-element.208, s32[]{:T(128)} %get-tuple-element.207, f32[3,1024]{1,0:T(4,128)S(1)} %get-tuple-element.215, s32[1024]{0:T(1024)S(1)} %bitcast.269), kind=kOutput, calls=%fused_computation.4.clone.1 | convolution fusion | flops 38797312 | bytes 36868 | tf_op jit(solution)/shard_map/while/body/eval_jaxpr/cn,kn->ck/dot_general | solution.py:160
  45.3 2.0 %fusion.321 = f32[8,3,1024]{2,1,0:T(4,128)S(1)} fusion(f32[8,3,1024]{2,1,0:T(4,128)S(1)} %get-tuple-element.208, s32[]{:T(128)} %get-tuple-element.207, f32[3,1024]{1,0:T(4,128)S(1)} %get-tuple-element.215, s32[1024]{0:T(1024)S(1)} %bitcast.269), kind=kOutput, calls=%fused_computation.4.clone.1 | convolution fusion | flops 38797312 | bytes 36868 | tf_op jit(solution)/shard_map/while/body/eval_jaxpr/cn,kn->ck/dot_general | solution.py:160
  47.3 2.0 %fusion.321 = f32[8,3,1024]{2,1,0:T(4,128)S(1)} fusion(f32[8,3,1024]{2,1,0:T(4,128)S(1)} %get-tuple-element.208, s32[]{:T(128)} %get-tuple-element.207, f32[3,1024]{1,0:T(4,128)S(1)} %get-tuple-element.215, s32[1024]{0:T(1024)S(1)} %bitcast.269), kind=kOutput, calls=%fused_computation.4.clone.1 | convolution fusion | flops 38797312 | bytes 36868 | tf_op jit(solution)/shard_map/while/body/eval_jaxpr/cn,kn->ck/dot_general | solution.py:160
  49.3 2.0 %fusion.321 = f32[8,3,1024]{2,1,0:T(4,128)S(1)} fusion(f32[8,3,1024]{2,1,0:T(4,128)S(1)} %get-tuple-element.208, s32[]{:T(128)} %get-tuple-element.207, f32[3,1024]{1,0:T(4,128)S(1)} %get-tuple-element.215, s32[1024]{0:T(1024)S(1)} %bitcast.269), kind=kOutput, calls=%fused_computation.4.clone.1 | convolution fusion | flops 38797312 | bytes 36868 | tf_op jit(solution)/shard_map/while/body/eval_jaxpr/cn,kn->ck/dot_general | solution.py:160
  51.4 0.6 copy-done.9
  52.4 0.6 collective-permute-start
  53.0 4.1 %collective-permute-start.1 = (f32[23,1,8,128]{3,2,1,0:T(8,128)S(1)}, f32[23,1,8,128]{3,2,1,0:T(8,128)S(1)}, u32[]{:S(2)}, u32[]{:S(2)}) collective-permute-start(f32[23,1,8,128]{3,2,1,0:T(8,128)S(1)} %get-tuple-element.133), channel_id=1, source_target_pairs={{4,0},{8,4},{12,8},{16,12},{20,16},{24,20},{28,24},{0,28},{5,1},{9... | collective-permute-start | bytes 282632 | tf_op jit(solution)/shard_map/ppermute | solution.py:47
  57.2 2.0 %fusion.10 = f32[7,1024]{1,0:T(8,128)S(1)} fusion(f32[7,1024]{1,0:T(8,128)S(1)} %reshape.445, s32[1024]{0:T(1024)S(1)} %bitcast.277), kind=kOutput, calls=%fused_computation.15 | convolution fusion | flops 89128960 | bytes 61440 | tf_op jit(solution)/shard_map/while/body/eval_jaxpr/cn,pn->cp/dot_general | solution.py:198
  59.3 0.6 multiply_subtract_fusion
  60.2 1.7 %collective-permute-start.3 = (f32[23,10,1,128]{3,2,1,0:T(1,128)S(1)}, f32[23,10,1,128]{3,2,1,0:T(1,128)S(1)}, u32[]{:S(2)}, u32[]{:S(2)}) collective-permute-start(f32[23,10,1,128]{3,2,1,0:T(1,128)S(1)} %get-tuple-element.130), channel_id=1, source_target_pairs={{1,0},{2,1},{3,2},{0,3},{5,4},{6,5},{7,6},{4,7},{9,8},{10,9},{11,1... | collective-permute-start | bytes 353288 | tf_op jit(solution)/shard_map/ppermute | solution.py:47
  62.3 2.6 %collective-permute-done.2 = f32[23,10,1,128]{3,2,1,0:T(1,128)S(1)} collective-permute-done((f32[23,10,1,128]{3,2,1,0:T(1,128)S(1)}, f32[23,10,1,128]{3,2,1,0:T(1,128)S(1)}, u32[]{:S(2)}, u32[]{:S(2)}) %collective-permute-start.2) | collective-permute-done | bytes 117792 | tf_op jit(solution)/shard_map/ppermute | solution.py:44
  64.9 0.4 fusion.16
  65.2 0.4 pad_maximum_fusion
  66.0 0.4 copy-done.7
  66.6 0.3 fusion.76
  67.1 0.5 fusion.88
  67.6 0.7 maximum_bitcast_fusion
  68.3 28.5 %while.26 = (s32[]{:T(128)}, f32[3,1024]{1,0:T(4,128)}, f32[8,3,1024]{2,1,0:T(4,128)}, s32[8,1024]{1,0:T(8,128)}, s32[]{:T(128)}, /*index=5*/s32[]{:T(128)}) while((s32[]{:T(128)}, f32[3,1024]{1,0:T(4,128)}, f32[8,3,1024]{2,1,0:T(4,128)}, s32[8,1024]{1,0:T(8,128)}, s32[]{:T(128)}, /*index=5*/s32[]{:T(128)}) %tuple.82), condition=%wide.region_6.7_spmd.clone, body=%wide.region_5.6_spmd.clone.sunk | while | flops 38803456 | bytes 57939 | solution.py:177
  68.3 0.8 constant_dynamic-slice_fusion.5
  69.1 2.8 %fusion.323 = f32[3,1024]{1,0:T(4,128)} fusion(s32[1024]{0:T(1024)S(1)} %bitcast.268, f32[3,1024]{1,0:T(4,128)} %get-tuple-element.224, f32[8,3,1024]{2,1,0:T(4,128)} %get-tuple-element.231, s32[]{:T(128)} %get-tuple-element.223, pred[]{:T(512)S(6)} %compare.3), kind=kOutput, calls=%fused_computation.9.clone.1 | convolution fusion | flops 38803456 | bytes 49665 | tf_op jit(solution)/shard_map/while/body/eval_jaxpr/ck,kn->cn/dot_general | solution.py:173
  71.9 0.8 constant_dynamic-slice_fusion.5
  72.7 2.8 %fusion.323 = f32[3,1024]{1,0:T(4,128)} fusion(s32[1024]{0:T(1024)S(1)} %bitcast.268, f32[3,1024]{1,0:T(4,128)} %get-tuple-element.224, f32[8,3,1024]{2,1,0:T(4,128)} %get-tuple-element.231, s32[]{:T(128)} %get-tuple-element.223, pred[]{:T(512)S(6)} %compare.3), kind=kOutput, calls=%fused_computation.9.clone.1 | convolution fusion | flops 38803456 | bytes 49665 | tf_op jit(solution)/shard_map/while/body/eval_jaxpr/ck,kn->cn/dot_general | solution.py:173
  75.5 0.8 constant_dynamic-slice_fusion.5
  76.2 2.8 %fusion.323 = f32[3,1024]{1,0:T(4,128)} fusion(s32[1024]{0:T(1024)S(1)} %bitcast.268, f32[3,1024]{1,0:T(4,128)} %get-tuple-element.224, f32[8,3,1024]{2,1,0:T(4,128)} %get-tuple-element.231, s32[]{:T(128)} %get-tuple-element.223, pred[]{:T(512)S(6)} %compare.3), kind=kOutput, calls=%fused_computation.9.clone.1 | convolution fusion | flops 38803456 | bytes 49665 | tf_op jit(solution)/shard_map/while/body/eval_jaxpr/ck,kn->cn/dot_general | solution.py:173
  79.0 0.8 constant_dynamic-slice_fusion.5
  79.8 2.8 %fusion.323 = f32[3,1024]{1,0:T(4,128)} fusion(s32[1024]{0:T(1024)S(1)} %bitcast.268, f32[3,1024]{1,0:T(4,128)} %get-tuple-element.224, f32[8,3,1024]{2,1,0:T(4,128)} %get-tuple-element.231, s32[]{:T(128)} %get-tuple-element.223, pred[]{:T(512)S(6)} %compare.3), kind=kOutput, calls=%fused_computation.9.clone.1 | convolution fusion | flops 38803456 | bytes 49665 | tf_op jit(solution)/shard_map/while/body/eval_jaxpr/ck,kn->cn/dot_general | solution.py:173
  82.6 0.8 constant_dynamic-slice_fusion.5
  83.3 2.8 %fusion.323 = f32[3,1024]{1,0:T(4,128)} fusion(s32[1024]{0:T(1024)S(1)} %bitcast.268, f32[3,1024]{1,0:T(4,128)} %get-tuple-element.224, f32[8,3,1024]{2,1,0:T(4,128)} %get-tuple-element.231, s32[]{:T(128)} %get-tuple-element.223, pred[]{:T(512)S(6)} %compare.3), kind=kOutput, calls=%fused_computation.9.clone.1 | convolution fusion | flops 38803456 | bytes 49665 | tf_op jit(solution)/shard_map/while/body/eval_jaxpr/ck,kn->cn/dot_general | solution.py:173
  86.1 0.8 constant_dynamic-slice_fusion.5
  86.9 2.8 %fusion.323 = f32[3,1024]{1,0:T(4,128)} fusion(s32[1024]{0:T(1024)S(1)} %bitcast.268, f32[3,1024]{1,0:T(4,128)} %get-tuple-element.224, f32[8,3,1024]{2,1,0:T(4,128)} %get-tuple-element.231, s32[]{:T(128)} %get-tuple-element.223, pred[]{:T(512)S(6)} %compare.3), kind=kOutput, calls=%fused_computation.9.clone.1 | convolution fusion | flops 38803456 | bytes 49665 | tf_op jit(solution)/shard_map/while/body/eval_jaxpr/ck,kn->cn/dot_general | solution.py:173
  89.7 0.8 constant_dynamic-slice_fusion.5
  90.5 2.8 %fusion.323 = f32[3,1024]{1,0:T(4,128)} fusion(s32[1024]{0:T(1024)S(1)} %bitcast.268, f32[3,1024]{1,0:T(4,128)} %get-tuple-element.224, f32[8,3,1024]{2,1,0:T(4,128)} %get-tuple-element.231, s32[]{:T(128)} %get-tuple-element.223, pred[]{:T(512)S(6)} %compare.3), kind=kOutput, calls=%fused_computation.9.clone.1 | convolution fusion | flops 38803456 | bytes 49665 | tf_op jit(solution)/shard_map/while/body/eval_jaxpr/ck,kn->cn/dot_general | solution.py:173
  93.3 0.8 constant_dynamic-slice_fusion.5
  94.0 2.8 %fusion.323 = f32[3,1024]{1,0:T(4,128)} fusion(s32[1024]{0:T(1024)S(1)} %bitcast.268, f32[3,1024]{1,0:T(4,128)} %get-tuple-element.224, f32[8,3,1024]{2,1,0:T(4,128)} %get-tuple-element.231, s32[]{:T(128)} %get-tuple-element.223, pred[]{:T(512)S(6)} %compare.3), kind=kOutput, calls=%fused_computation.9.clone.1 | convolution fusion | flops 38803456 | bytes 49665 | tf_op jit(solution)/shard_map/while/body/eval_jaxpr/ck,kn->cn/dot_general | solution.py:173
  96.8 0.8 reshape.444
  97.6 0.7 copy.52
  98.3 5.5 %all-to-all-start.2 = ((f32[3,32,32]{2,0,1:T(4,128)}), f32[3,32,32]{2,0,1:T(4,128)S(1)}, u32[]{:S(2)}, u32[]{:S(2)}) async-start(f32[3,32,32]{2,0,1:T(4,128)} %copy.52), calls=%async_computation.2 | async-start | bytes 131072 | tf_op jit(solution)/shard_map/all_to_all | solution.py:180
  104.0 0.6 copy-done.4
  106.5 0.9 broadcast_select_fusion
  107.4 3.8 %all-to-all-done.2 = f32[3,32,32]{2,0,1:T(4,128)S(1)} async-done(((f32[3,32,32]{2,0,1:T(4,128)}), f32[3,32,32]{2,0,1:T(4,128)S(1)}, u32[]{:S(2)}, u32[]{:S(2)}) %all-to-all-start.2) | async-done | bytes 12320 | tf_op jit(solution)/shard_map/all_to_all | solution.py:180
  111.2 0.8 fusion.17
  112.1 1.4 %fusion.278 = (f32[3,512]{1,0:T(4,128)}, f32[3,512]{1,0:T(4,128)}) fusion(f32[3,512]{1,0:T(4,128)S(1)} %copy-done.27, f32[3,512]{1,0:T(4,128)S(1)} %copy-done.25, f32[512]{0:T(512)S(1)} %copy-done.29, f32[3,512]{1,0:T(4,128)S(1)} %fusion.17, s32[1024]{0:T(1024)S(1)} %bitcast.276, f32[1024]{0:T(1024)S(1)} %bitcast.274, f32[1024]{0:T(1024)S(1)} %copy-done.16, ...), kind=kOutput, calls=%fused_computation.545 | convolution fusion | flops 19414016 | bytes 83968 | tf_op jit(solution)/shard_map/while/body/eval_jaxpr/cp,pg->cg/dot_general | solution.py:202
  (118 shorter events, 4.6 us)
Async XLA Ops:
  0.6 14.7 %copy-start.23 = (f32[19]{0:T(128)S(1)}, f32[19]{0:T(128)}, u32[]{:S(2)}) copy-start(f32[19]{0:T(128)} %constant.45.clone) | copy-start | bytes 232
  0.6 14.7 %copy-start = (f32[19,8,8,128]{3,2,1,0:T(8,128)S(1)}, f32[19,8,8,128]{3,2,1,0:T(8,128)}, u32[]{:S(2)}) copy-start(f32[19,8,8,128]{3,2,1,0:T(8,128)} %param.14) | copy-start | bytes 1867780
  3.2 14.4 %all-to-all-start = ((s32[32,1,32]{2,1,0:T(1,128)}), s32[32,1,32]{2,1,0:T(1,128)S(1)}, u32[]{:S(2)}, u32[]{:S(2)}) async-start(s32[32,1,32]{2,1,0:T(1,128)} %all_to_all.12), calls=%async_computation | async-start | bytes 32768 | tf_op jit(solution)/shard_map/all_to_all | solution.py:143
  13.7 3.2 %copy-start.10 = (s32[8,8,128]{2,1,0:T(8,128)S(1)}, s32[8,8,128]{2,1,0:T(8,128)}, u32[]{:S(2)}) copy-start(s32[8,8,128]{2,1,0:T(8,128)} %param.15) | copy-start | bytes 98308
  13.7 3.8 %copy-start.19 = (s32[2,1024]{1,0:T(2,128)S(1)}, s32[2,1024]{1,0:T(2,128)}, u32[]{:S(2)}) copy-start(s32[2,1024]{1,0:T(2,128)} %param.17) | copy-start | bytes 24580
  13.7 4.0 %copy-start.24 = (f32[3,512]{1,0:T(4,128)S(1)}, f32[3,512]{1,0:T(4,128)}, u32[]{:S(2)}) copy-start(f32[3,512]{1,0:T(4,128)} %param.19) | copy-start | bytes 18436
  13.7 4.0 %copy-start.26 = (f32[3,512]{1,0:T(4,128)S(1)}, f32[3,512]{1,0:T(4,128)}, u32[]{:S(2)}) copy-start(f32[3,512]{1,0:T(4,128)} %param.18) | copy-start | bytes 18436
  13.7 4.0 %copy-start.28 = (f32[512]{0:T(512)S(1)}, f32[512]{0:T(512)}, u32[]{:S(2)}) copy-start(f32[512]{0:T(512)} %param.20) | copy-start | bytes 6148
  17.5 8.9 %copy-start.21 = (s32[1,1024]{1,0:T(1,128)}, s32[1,1024]{1,0:T(1,128)S(1)}, u32[]{:S(2)}) copy-start(s32[1,1024]{1,0:T(1,128)S(1)} %get-tuple-element.145) | copy-start | bytes 12292
  17.6 16.5 %copy-start.17 = (s32[32,1,32]{2,1,0:T(1,128)}, s32[32,1,32]{2,1,0:T(1,128)S(1)}, u32[]{:S(2)}) copy-start(s32[32,1,32]{2,1,0:T(1,128)S(1)} %all-to-all-done) | copy-start | bytes 12292
  20.6 13.0 %all-to-all-start.1 = ((f32[32,1,224]{2,1,0:T(1,128)}), f32[32,1,224]{2,1,0:T(1,128)S(1)}, u32[]{:S(2)}, u32[]{:S(2)}) async-start(f32[32,1,224]{2,1,0:T(1,128)} %reshape.459), calls=%async_computation.1 | async-start | bytes 65536 | tf_op jit(solution)/shard_map/all_to_all | solution.py:152
  27.4 31.9 %copy-start.11 = (f32[7,1024]{1,0:T(8,128)}, f32[7,1024]{1,0:T(8,128)S(1)}, u32[]{:S(2)}) copy-start(f32[7,1024]{1,0:T(8,128)S(1)} %fusion.13) | copy-start | bytes 86020
  51.4 0.6 copy-start.9
  52.4 7.6 %collective-permute-start = (f32[23,1,8,128]{3,2,1,0:T(8,128)S(1)}, f32[23,1,8,128]{3,2,1,0:T(8,128)S(1)}, u32[]{:S(2)}, u32[]{:S(2)}) collective-permute-start(f32[23,1,8,128]{3,2,1,0:T(8,128)S(1)} %get-tuple-element.134), channel_id=1, source_target_pairs={{0,4},{4,8},{8,12},{12,16},{16,20},{20,24},{24,28},{28,0},{1,5},{5... | collective-permute-start | bytes 282632 | tf_op jit(solution)/shard_map/ppermute | solution.py:44
  53.0 7.0 %collective-permute-start.1 = (f32[23,1,8,128]{3,2,1,0:T(8,128)S(1)}, f32[23,1,8,128]{3,2,1,0:T(8,128)S(1)}, u32[]{:S(2)}, u32[]{:S(2)}) collective-permute-start(f32[23,1,8,128]{3,2,1,0:T(8,128)S(1)} %get-tuple-element.133), channel_id=1, source_target_pairs={{4,0},{8,4},{12,8},{16,12},{20,16},{24,20},{28,24},{0,28},{5,1},{9... | collective-permute-start | bytes 282632 | tf_op jit(solution)/shard_map/ppermute | solution.py:47
  59.2 2.8 %copy-start.13 = (f32[7,1024]{1,0:T(8,128)}, f32[7,1024]{1,0:T(8,128)S(1)}, u32[]{:S(2)}) copy-start(f32[7,1024]{1,0:T(8,128)S(1)} %fusion.10) | copy-start | bytes 86020
  59.3 2.8 %copy-start.15 = (f32[1024]{0:T(1024)}, f32[1024]{0:T(1024)S(1)}, u32[]{:S(2)}) copy-start(f32[1024]{0:T(1024)S(1)} %get-tuple-element.147) | copy-start | bytes 12292
  60.1 4.8 %collective-permute-start.2 = (f32[23,10,1,128]{3,2,1,0:T(1,128)S(1)}, f32[23,10,1,128]{3,2,1,0:T(1,128)S(1)}, u32[]{:S(2)}, u32[]{:S(2)}) collective-permute-start(f32[23,10,1,128]{3,2,1,0:T(1,128)S(1)} %get-tuple-element.129), channel_id=1, source_target_pairs={{0,1},{1,2},{2,3},{3,0},{4,5},{5,6},{6,7},{7,4},{8,9},{9,10},{10,1... | collective-permute-start | bytes 353288 | tf_op jit(solution)/shard_map/ppermute | solution.py:44
  60.2 4.7 %collective-permute-start.3 = (f32[23,10,1,128]{3,2,1,0:T(1,128)S(1)}, f32[23,10,1,128]{3,2,1,0:T(1,128)S(1)}, u32[]{:S(2)}, u32[]{:S(2)}) collective-permute-start(f32[23,10,1,128]{3,2,1,0:T(1,128)S(1)} %get-tuple-element.130), channel_id=1, source_target_pairs={{1,0},{2,1},{3,2},{0,3},{5,4},{6,5},{7,6},{4,7},{9,8},{10,9},{11,1... | collective-permute-start | bytes 353288 | tf_op jit(solution)/shard_map/ppermute | solution.py:47
  65.6 0.7 copy-start.7
  66.3 0.8 copy-start.1
  66.3 0.8 copy-start.3
  66.3 0.8 copy-start.5
  98.3 12.9 %all-to-all-start.2 = ((f32[3,32,32]{2,0,1:T(4,128)}), f32[3,32,32]{2,0,1:T(4,128)S(1)}, u32[]{:S(2)}, u32[]{:S(2)}) async-start(f32[3,32,32]{2,0,1:T(4,128)} %copy.52), calls=%async_computation.2 | async-start | bytes 131072 | tf_op jit(solution)/shard_map/all_to_all | solution.py:180
  103.8 0.8 copy-start.4
  103.8 0.8 copy-start.6
  103.9 0.8 copy-start.2
  105.7 0.8 copy-start.8
  106.0 5.3 %copy-start.18 = (s32[32,1,32]{2,1,0:T(1,128)S(1)}, s32[32,1,32]{2,1,0:T(1,128)}, u32[]{:S(2)}) copy-start(s32[32,1,32]{2,1,0:T(1,128)} %copy-done.17) | copy-start | bytes 12292
  106.2 5.9 %copy-start.12 = (f32[7,1024]{1,0:T(8,128)S(1)}, f32[7,1024]{1,0:T(8,128)}, u32[]{:S(2)}) copy-start(f32[7,1024]{1,0:T(8,128)} %copy-done.11) | copy-start | bytes 86020
  106.2 5.9 %copy-start.14 = (f32[7,1024]{1,0:T(8,128)S(1)}, f32[7,1024]{1,0:T(8,128)}, u32[]{:S(2)}) copy-start(f32[7,1024]{1,0:T(8,128)} %copy-done.13) | copy-start | bytes 86020
  106.2 5.9 %copy-start.16 = (f32[1024]{0:T(1024)S(1)}, f32[1024]{0:T(1024)}, u32[]{:S(2)}) copy-start(f32[1024]{0:T(1024)} %copy-done.15) | copy-start | bytes 12292
  106.2 5.9 %copy-start.20 = (f32[1,1024]{1,0:T(1,128)S(1)}, f32[1,1024]{1,0:T(1,128)}, u32[]{:S(2)}) copy-start(f32[1,1024]{1,0:T(1,128)} %multiply_subtract_fusion) | copy-start | bytes 12292
  106.2 5.9 %copy-start.22 = (s32[1,1024]{1,0:T(1,128)S(1)}, s32[1,1024]{1,0:T(1,128)}, u32[]{:S(2)}) copy-start(s32[1,1024]{1,0:T(1,128)} %copy-done.21) | copy-start | bytes 12292
  106.2 5.9 %copy-start.25 = (f32[3,512]{1,0:T(4,128)S(1)}, f32[3,512]{1,0:T(4,128)}, u32[]{:S(2)}) copy-start(f32[3,512]{1,0:T(4,128)} %param.19) | copy-start | bytes 18436
  106.2 5.9 %copy-start.27 = (f32[3,512]{1,0:T(4,128)S(1)}, f32[3,512]{1,0:T(4,128)}, u32[]{:S(2)}) copy-start(f32[3,512]{1,0:T(4,128)} %param.18) | copy-start | bytes 18436
  106.3 5.9 %copy-start.29 = (f32[512]{0:T(512)S(1)}, f32[512]{0:T(512)}, u32[]{:S(2)}) copy-start(f32[512]{0:T(512)} %param.21) | copy-start | bytes 6148
where the time goes:
time: 115 us; the launch traced here: 114 us
  matrix products  49.5 us (43%)
  starting transfers between devices  25.2 us (22%)
  local copies, waits for them, and re-layouts  14.4 us (13%)
  waiting for transfers between devices  12.7 us (11%)
  other arithmetic  10.4 us (9%)
  between operations  1.27 us (1%)
    dot_general x8, matrix products, add_plane(): jnp.einsum('ck,kn->cn', forces, indicator(ids, near_count), precision=hig...  22.4 us
    dot_general x8, matrix products, wall_plane(): jnp.einsum('cn,kn->ck', near_wall, indicator(ids, near_count), precision=...  16.1 us
    all_to_all x1, starting transfers between devices, local(): lax.all_to_all(near_rows.reshape(devices, slot_count), ('gx', 'yz'), spli...  7.33 us
    dynamic_slice x16, local copies, waits for them, and re-layouts, local(): lax.map(wall_plane, plane_ids)  6.25 us
    all_to_all x1, waiting for transfers between devices, local(): lax.all_to_all(answer, ('gx', 'yz'), split_axis=1, concat_axis=1, tiled=T...  6.14 us
    ppermute x2, starting transfers between devices, extended(): lax.ppermute(lax.slice_in_dim(block, 0, width, axis=dim), axis, backward)  5.88 us
    all_to_all x1, starting transfers between devices, local(): lax.all_to_all(answer, ('gx', 'yz'), split_axis=1, concat_axis=1, tiled=T...  5.74 us
    all_to_all x1, starting transfers between devices, local(): lax.all_to_all(slot_force.reshape(3, devices, slot_count), ('gx', 'yz'),...  5.53 us
  transfers between devices with their start and end apart: 7, of which 4 were waited for; matrix products, arithmetic and copies ran while one was open for 12% of the time, Pallas kernels for 0%

commit v1 on v0

v1 whole, which is shorter than its diff:
```python
import functools

import jax
import jax.numpy as jnp
from jax import lax
from jax.experimental import pallas as pl
from jax.experimental.pallas import tpu as pltpu
from jax.sharding import PartitionSpec as P

lattice_dirs = (
    (0, 0, 0),
    (1, 0, 0),
    (-1, 0, 0),
    (0, 1, 0),
    (0, -1, 0),
    (0, 0, 1),
    (0, 0, -1),
    (1, 1, 0),
    (-1, -1, 0),
    (1, -1, 0),
    (-1, 1, 0),
    (1, 0, 1),
    (-1, 0, -1),
    (1, 0, -1),
    (-1, 0, 1),
    (0, 1, 1),
    (0, -1, -1),
    (0, 1, -1),
    (0, -1, 1),
)
lattice_weights = (1.0 / 3.0,) + (1.0 / 18.0,) * 6 + (1.0 / 36.0,) * 12
opposite = (0, 2, 1, 4, 3, 6, 5, 8, 7, 10, 9, 12, 11, 14, 13, 16, 15, 18, 17)
relax_rate = 1.25
stiffness = 0.5
damping = 0.5

still = (0, 3, 4, 5, 6, 15, 16, 17, 18)
ahead = (1, 7, 9, 11, 13)
behind = (2, 8, 10, 12, 14)
channel = {}
for place, name in enumerate(still + ahead):
    channel[name] = place
RHO = len(still) + len(ahead)
for place, name in enumerate(behind):
    channel[name] = RHO + 1 + place
CHANNELS = RHO + 1 + len(behind)
X_LOW = len(still)
rise = (3, 15, 17, 7, 19, 10)
fall = (4, 16, 18, 8, 19, 9)
channel[19] = RHO
FACE = 6
SUB = 8
LANE = 128


def project(direction, parts):
    total = None
    for compo in range(3):
        factor = lattice_dirs[direction][compo]
        if factor != 0:
            term = parts[compo] if factor > 0 else -parts[compo]
            total = term if total is None else total + term
    return total


def lookup(row, lanes):
    table = jnp.broadcast_to(row, lanes.shape)
    return jnp.take_along_axis(table, lanes, axis=1, mode="promise_in_bounds")


def lane_roll(value, shift):
    shift = shift % LANE
    return value if shift == 0 else pltpu.roll(value, shift, 1)


def sums_by_entry(parts, rows, lanes):
    sub = lax.broadcasted_iota(jnp.int32, (SUB, LANE), 0)
    tall = lax.broadcasted_iota(jnp.int32, (LANE, LANE), 0)
    left = [[] for part in parts]
    right = []
    for y in range(SUB):
        hit = jnp.broadcast_to(rows[y : y + 1], (SUB, LANE)) == sub
        for which, part in enumerate(parts):
            spread = jnp.broadcast_to(part[y : y + 1], (SUB, LANE))
            left[which].append(jnp.where(hit, spread, 0.0))
        match = jnp.broadcast_to(lanes[y : y + 1], (LANE, LANE)) == tall
        right.append(jnp.where(match, 1.0, 0.0).astype(jnp.bfloat16))
    wide = [jnp.concatenate(pieces, axis=1) for pieces in left]
    wide.append(jnp.zeros_like(wide[0]))
    full = jnp.concatenate(wide, axis=0)
    first = full.astype(jnp.bfloat16)
    rest = full - first.astype(jnp.float32)
    second = rest.astype(jnp.bfloat16)
    third = (rest - second.astype(jnp.float32)).astype(jnp.bfloat16)
    table = jnp.concatenate(right, axis=1)
    total = lax.dot_general(
        jnp.concatenate([first, second, third], axis=0),
        table,
        (((1,), (1,)), ((), ())),
        preferred_element_type=jnp.float32,
    )
    return total[0:32] + total[32:64] + total[64:96]


def contact_push(pos_a, vel_a, rad_a, pos_b, vel_b, rad_b):
    offset = [a - b for a, b in zip(pos_a, pos_b)]
    length = jnp.sqrt(offset[0] * offset[0] + offset[1] * offset[1] + offset[2] * offset[2])
    scale = jnp.maximum(length, 1.0)
    normal = [part / scale for part in offset]
    intersection = jnp.maximum(rad_a + rad_b - length, 0.0)
    closing = (
        (vel_a[0] - vel_b[0]) * normal[0]
        + (vel_a[1] - vel_b[1]) * normal[1]
        + (vel_a[2] - vel_b[2]) * normal[2]
    )
    amount = stiffness * intersection - damping * intersection * closing
    return [amount * part for part in normal]


def kernel(
    count_x,
    count_y,
    slot,
    pops,
    cells,
    near,
    pairs,
    position,
    velocity,
    radius,
    mass,
    out_pops,
    out_vel,
    out_pos,
    asked,
    reply,
    known,
    sent_force,
    got_force,
    table,
    wall,
    low_src,
    high_src,
    low_rows,
    high_rows,
    pair_ids,
    send_sems,
    recv_sems,
    halo_send,
    halo_recv,
):
    devices = count_x * count_y
    groups = devices // SUB
    per_row = LANE // slot
    width = pops.shape[1]
    owned = position.shape[1]
    banks = owned // LANE
    at_x = lax.axis_index("gx")
    at_y = lax.axis_index("yz")
    me = at_x * count_y + at_y
    sub = lax.broadcasted_iota(jnp.int32, (SUB, LANE), 0)
    lane = lax.broadcasted_iota(jnp.int32, (SUB, LANE), 1)

    def peer_of(step):
        peer = lax.rem(me + step, devices)
        return peer, (peer // count_y, lax.rem(peer, count_y))

    barrier = pltpu.get_barrier_semaphore()

    def greet(step, carry):
        peer, where = peer_of(step)
        pl.semaphore_signal(
            barrier, inc=1, device_id=where, device_id_type=pl.DeviceIdType.MESH
        )
        return carry

    lax.fori_loop(1, devices, greet, 0)
    asked[pl.ds(me, 1)] = near[pl.ds(me // per_row, 1)]
    pl.semaphore_wait(barrier, devices - 1)

    def everyone(source_of, target, which):
        def start(step, carry):
            peer, where = peer_of(step)
            pltpu.make_async_remote_copy(
                src_ref=source_of(peer),
                dst_ref=target.at[pl.ds(me, 1)],
                send_sem=send_sems.at[which],
                recv_sem=recv_sems.at[which],
                device_id=where,
                device_id_type=pl.DeviceIdType.MESH,
            ).start()
            return carry

        lax.fori_loop(1, devices, start, 0)

    def arrived(target, sems, which):
        part = target.at[pl.ds(0, devices - 1)]
        pltpu.make_async_copy(part, part, sems.at[which]).wait()

    everyone(lambda peer: near.at[pl.ds(peer // per_row, 1)], asked, 0)

    def collide(x, carry):
        values = [pops[i, x] for i in range(19)]
        density = values[0]
        for i in range(1, 19):
            density = density + values[i]
        scale = 1.0 / density
        speeds = []
        for compo in range(3):
            moment = None
            for i in range(19):
                factor = lattice_dirs[i][compo]
                if factor != 0:
                    if moment is None:
                        moment = values[i]
                    elif factor > 0:
                        moment = moment + values[i]
                    else:
                        moment = moment - values[i]
            speeds.append(moment * scale)
        square = speeds[0] * speeds[0] + speeds[1] * speeds[1] + speeds[2] * speeds[2]
        base = 1.0 - 1.5 * square
        weighted = {w: (relax_rate * w) * density for w in set(lattice_weights)}
        keep = 1.0 - relax_rate
        fresh = keep * values[0] + weighted[lattice_weights[0]] * base
        table[channel[0], x + 1] = fresh
        after = fresh
        for i in range(1, 19, 2):
            along = project(i, speeds)
            even = base + 4.5 * along * along
            odd = 3.0 * along
            gain = weighted[lattice_weights[i]]
            plus = keep * values[i] + gain * (even + odd)
            minus = keep * values[i + 1] + gain * (even - odd)
            table[channel[i], x + 1] = plus
            table[channel[i + 1], x + 1] = minus
            after = after + plus + minus
        table[RHO, x + 1] = jnp.where(cells[x] >= 0, 0.0, after)
        return carry

    lax.fori_loop(0, width, collide, 0)

    arrived(asked, recv_sems, 0)
    quarter = lax.rem(me, per_row)
    field = lane // slot
    within = lane - field * slot
    wanted = []
    for q in range(groups):
        ask = asked[q * SUB : (q + 1) * SUB, 0, :]
        row = jnp.take_along_axis(
            ask, within + quarter * slot, axis=1, mode="promise_in_bounds"
        )
        wanted.append(row)
        safe = jnp.maximum(row, 0)
        bank = safe // LANE
        spot = safe - bank * LANE
        vel_row = jnp.zeros((SUB, LANE), jnp.float32)
        pos_row = jnp.zeros((SUB, LANE), jnp.float32)
        for h in range(banks):
            span = slice(h * LANE, (h + 1) * LANE)
            for compo in range(3):
                mine = (bank == h) & (field == compo)
                vel_row = jnp.where(mine, lookup(velocity[compo : compo + 1, span], spot), vel_row)
                pos_row = jnp.where(mine, lookup(position[compo : compo + 1, span], spot), pos_row)
            mine = (bank == h) & (field == 3)
            pos_row = jnp.where(mine, lookup(radius[0:1, span], spot), pos_row)
        reply[q * SUB : (q + 1) * SUB, 0, :] = vel_row
        reply[q * SUB : (q + 1) * SUB, 1, :] = pos_row
    everyone(lambda peer: reply.at[pl.ds(peer, 1)], known, 1)

    part_of_lane = lane // slot

    def to_table(read, compo):
        value = jnp.zeros((SUB, LANE), jnp.float32)
        for q in range(groups):
            moved = lane_roll(read(q), (q - compo) * slot)
            value = jnp.where(part_of_lane == q, moved, value)
        return value

    wanted_table = jnp.zeros((SUB, LANE), jnp.int32)
    for q in range(groups):
        wanted_table = jnp.where(part_of_lane == q, lane_roll(wanted[q], q * slot), wanted_table)
    wanted_bank = wanted_table // LANE
    wanted_bank = jnp.where(wanted_table < 0, SUB, wanted_bank)
    wanted_spot = jnp.bitwise_and(wanted_table, LANE - 1)

    arrived(known, recv_sems, 1)
    known[pl.ds(me, 1)] = reply[pl.ds(me, 1)]
    vel_table = [
        to_table(lambda q: known[q * SUB : (q + 1) * SUB, 0, :], compo) for compo in range(3)
    ]
    vel_rows = [[part[r : r + 1] for r in range(SUB)] for part in vel_table]

    def entry(ids):
        owner = ids // slot
        inner = ids - owner * slot
        row = jnp.bitwise_and(owner, SUB - 1)
        return row, (owner // SUB) * slot + inner

    def from_table(rows_of, row, spot):
        value = jnp.zeros((SUB, LANE), jnp.float32)
        for r in range(SUB):
            value = jnp.where(row == r, lookup(rows_of[r], spot), value)
        return value

    def fill_walls(x, carry):
        ids = cells[x]
        solid = ids >= 0
        row, spot = entry(jnp.maximum(ids, 0))
        speeds = [from_table(rows_of, row, spot) for rows_of in vel_rows]
        for compo in range(3):
            wall[compo, x] = speeds[compo]
        for i in range(1, 19, 2):
            motion = (6.0 * lattice_weights[i]) * project(i, speeds)
            plus = jnp.where(solid, motion, table[channel[i], x + 1])
            minus = jnp.where(solid, -motion, table[channel[i + 1], x + 1])
            table[channel[i], x + 1] = plus
            table[channel[i + 1], x + 1] = minus
            for which, value in ((i, plus), (i + 1, minus)):
                if which in rise:
                    high_src[rise.index(which), pl.ds(x, 1)] = value[SUB - 1 : SUB][None]
                if which in fall:
                    low_src[fall.index(which), pl.ds(x, 1)] = value[0:1][None]
        rho = table[RHO, x + 1]
        high_src[4, pl.ds(x, 1)] = rho[SUB - 1 : SUB][None]
        low_src[4, pl.ds(x, 1)] = rho[0:1][None]
        return carry

    lax.fori_loop(0, width, fill_walls, 0)

    right = lax.rem(at_x + 1, count_x)
    left = lax.rem(at_x + count_x - 1, count_x)
    upper = lax.rem(at_y + 1, count_y)
    lower = lax.rem(at_y + count_y - 1, count_y)
    end = width - 1
    hops = (
        (table.at[X_LOW : X_LOW + FACE, width], table.at[X_LOW : X_LOW + FACE, 0], right, at_y),
        (table.at[RHO : RHO + FACE, 1], table.at[RHO : RHO + FACE, width + 1], left, at_y),
        (high_src, low_rows.at[:, 1 : width + 1], at_x, upper),
        (low_src, high_rows.at[:, 1 : width + 1], at_x, lower),
        (high_src.at[3:5, end], low_rows.at[3:5, 0], right, upper),
        (high_src.at[4:6, 0], low_rows.at[4:6, width + 1], left, upper),
        (low_src.at[3:5, 0], high_rows.at[3:5, width + 1], left, lower),
        (low_src.at[4:6, end], high_rows.at[4:6, 0], right, lower),
    )
    copies = []
    for which, (source, target, to_x, to_y) in enumerate(hops):
        copy = pltpu.make_async_remote_copy(
            src_ref=source,
            dst_ref=target,
            send_sem=halo_send.at[which],
            recv_sem=halo_recv.at[which],
            device_id=(to_x, to_y),
            device_id_type=pl.DeviceIdType.MESH,
        )
        copy.start()
        copies.append(copy)

    for y in range(SUB):
        pair_ids[0, y : y + 1] = pairs[0:1, y * LANE : (y + 1) * LANE]
        pair_ids[1, y : y + 1] = pairs[1:2, y * LANE : (y + 1) * LANE]
    first = pair_ids[0]
    first_bank = first // LANE
    first_spot = first - first_bank * LANE

    def from_owned(ref, compo):
        value = jnp.zeros((SUB, LANE), jnp.float32)
        for h in range(banks):
            part = lookup(ref[compo : compo + 1, h * LANE : (h + 1) * LANE], first_spot)
            value = jnp.where(first_bank == h, part, value)
        return value

    row, spot = entry(pair_ids[1])

    def from_known(field_table):
        return from_table([field_table[r : r + 1] for r in range(SUB)], row, spot)

    pos_table = [
        to_table(lambda q: known[q * SUB : (q + 1) * SUB, 1, :], compo) for compo in range(4)
    ]
    push = contact_push(
        [from_owned(position, compo) for compo in range(3)],
        [from_owned(velocity, compo) for compo in range(3)],
        from_owned(radius, 0),
        [from_known(pos_table[compo]) for compo in range(3)],
        [from_known(vel_table[compo]) for compo in range(3)],
        from_known(pos_table[3]),
    )
    contact = sums_by_entry(push, first_bank, first_spot)

    for copy in copies:
        copy.wait()

    def stream(x, total):
        solid = cells[x] >= 0
        here_rho = table[RHO, x + 1]
        speeds = [wall[compo, x] for compo in range(3)]
        out_pops[0, x] = jnp.where(solid, pops[0, x], table[channel[0], x + 1])
        rows_made = {}

        def moved(name, shift_x, shift_y, shift_z):
            key = (name, shift_x, shift_y, 0)
            at = x + 1 - shift_x
            if key not in rows_made:
                value = table[channel[name], at]
                if shift_y > 0:
                    edge = jnp.broadcast_to(low_rows[rise.index(name), at], (SUB, LANE))
                    value = jnp.where(sub == 0, edge, pltpu.roll(value, 1, 0))
                elif shift_y < 0:
                    edge = jnp.broadcast_to(high_rows[fall.index(name), at], (SUB, LANE))
                    value = jnp.where(sub == SUB - 1, edge, pltpu.roll(value, SUB - 1, 0))
                rows_made[key] = value
            if shift_z == 0:
                return rows_made[key]
            deep = (name, shift_x, shift_y, shift_z)
            if deep not in rows_made:
                rows_made[deep] = lane_roll(rows_made[key], shift_z)
            return rows_made[deep]

        force = [jnp.zeros((SUB, LANE), jnp.float32) for compo in range(3)]
        for i in range(1, 19):
            shift = lattice_dirs[i]
            source = moved(i, *shift)
            rho = moved(19, *shift)
            fluid = rho > 0.0
            bounce = table[channel[opposite[i]], x + 1] + here_rho * source
            fresh = jnp.where(fluid, source, bounce)
            out_pops[i, x] = jnp.where(solid, pops[i, x], fresh)
            drag = rho * ((6.0 * lattice_weights[i]) * project(i, speeds))
            link = jnp.where(fluid, 2.0 * source - drag, 0.0)
            for compo in range(3):
                if shift[compo] > 0:
                    force[compo] = force[compo] + link
                elif shift[compo] < 0:
                    force[compo] = force[compo] - link
        force = [jnp.where(solid, part, 0.0) for part in force]
        where = entry(jnp.maximum(cells[x], 0))
        return total + sums_by_entry(force, *where)

    slot_force = lax.fori_loop(0, width, stream, jnp.zeros((32, LANE), jnp.float32))

    for q in range(groups):
        value = jnp.zeros((SUB, LANE), jnp.float32)
        for compo in range(3):
            part = lane_roll(slot_force[compo * SUB : (compo + 1) * SUB], (compo - q) * slot)
            value = jnp.where(field == compo, part, value)
        sent_force[q * SUB : (q + 1) * SUB, 0, :] = value
    everyone(lambda peer: sent_force.at[pl.ds(peer, 1)], got_force, 2)
    arrived(asked, send_sems, 0)
    arrived(reply, send_sems, 1)
    arrived(got_force, recv_sems, 2)
    got_force[pl.ds(me, 1)] = sent_force[pl.ds(me, 1)]
    gained = [
        to_table(lambda q: got_force[q * SUB : (q + 1) * SUB, 0, :], compo) for compo in range(3)
    ]
    fluid_force = sums_by_entry(gained, wanted_bank, wanted_spot)
    force = fluid_force + contact
    for compo in range(3):
        for h in range(banks):
            span = slice(h * LANE, (h + 1) * LANE)
            line = compo * SUB + h
            speed = velocity[compo : compo + 1, span] + force[line : line + 1] / mass[0:1, span]
            out_vel[compo : compo + 1, span] = speed
            out_pos[compo : compo + 1, span] = position[compo : compo + 1, span] + speed
    arrived(sent_force, send_sems, 2)


def local(
    populations,
    cell_grain,
    near_rows,
    contact_pairs,
    grain_position,
    grain_velocity,
    grain_radius,
    grain_mass,
):
    count_x = lax.axis_size("gx")
    count_y = lax.axis_size("yz")
    devices = count_x * count_y
    near_count = near_rows.shape[1]
    slot = near_count // devices
    owned = grain_position.shape[1]
    width = populations.shape[1]
    near_lines = near_rows.reshape(near_count // LANE, 1, LANE)
    whole = pl.BlockSpec(memory_space=pltpu.VMEM)
    f32 = jnp.float32
    return pl.pallas_call(
        functools.partial(kernel, count_x, count_y, slot),
        out_shape=(
            jax.ShapeDtypeStruct(populations.shape, f32),
            jax.ShapeDtypeStruct(grain_velocity.shape, f32),
            jax.ShapeDtypeStruct(grain_position.shape, f32),
        ),
        in_specs=[whole] * 8,
        out_specs=(whole,) * 3,
        scratch_shapes=[
            pltpu.VMEM((devices, 1, LANE), jnp.int32),
            pltpu.VMEM((devices, 2, LANE), f32),
            pltpu.VMEM((devices, 2, LANE), f32),
            pltpu.VMEM((devices, 1, LANE), f32),
            pltpu.VMEM((devices, 1, LANE), f32),
            pltpu.VMEM((CHANNELS, width + 2, SUB, LANE), f32),
            pltpu.VMEM((3, width, SUB, LANE), f32),
            pltpu.VMEM((FACE, width, 1, LANE), f32),
            pltpu.VMEM((FACE, width, 1, LANE), f32),
            pltpu.VMEM((FACE, width + 2, 1, LANE), f32),
            pltpu.VMEM((FACE, width + 2, 1, LANE), f32),
            pltpu.VMEM((2, SUB, LANE), jnp.int32),
            pltpu.SemaphoreType.DMA((3,)),
            pltpu.SemaphoreType.DMA((3,)),
            pltpu.SemaphoreType.DMA((8,)),
            pltpu.SemaphoreType.DMA((8,)),
        ],
        compiler_params=pltpu.CompilerParams(collective_id=0, has_side_effects=True),
        name="step",
    )(
        populations,
        cell_grain,
        near_lines,
        contact_pairs,
        grain_position,
        grain_velocity,
        grain_radius.reshape(1, owned),
        grain_mass.reshape(1, owned),
    )


def solution(mesh):
    return jax.shard_map(
        local,
        mesh=mesh,
        in_specs=(
            P(None, "gx", "yz", None),
            P("gx", "yz", None),
            P(("gx", "yz"), None),
            P(None, ("gx", "yz")),
            P(None, ("gx", "yz")),
            P(None, ("gx", "yz")),
            P(("gx", "yz")),
            P(("gx", "yz")),
        ),
        out_specs=(P(None, "gx", "yz", None), P(None, ("gx", "yz")), P(None, ("gx", "yz"))),
        check_vma=False,
    )
```

time: 115 us -> 35 us (0.30); the launches traced: 114 us -> 34.8 us
  matrix products: 49.5 us -> 0 us
  Pallas kernels: 0 us -> 30.9 us
  starting transfers between devices: 25.2 us -> 0 us
  waiting for transfers between devices: 12.7 us -> 0 us
  local copies, waits for them, and re-layouts: 14.4 us -> 3.27 us
  other arithmetic: 10.4 us -> 0 us
    dot_general x23 -> x0, matrix products: 49.5 us -> none  [the longest x8 22.4 us: add_plane(): jnp.einsum('ck,kn->cn', forces, indicator(ids, near_count), precision=hig...]
    pallas_call x0 -> x1, Pallas kernels: none -> 30.9 us  [local(): pl.pallas_call(functools.partial(kernel, count_x, count_y, slot), out_sha...]
    all_to_all x3 -> x0, starting transfers between devices: 18.6 us -> none  [the longest x1 7.33 us: local(): lax.all_to_all(near_rows.reshape(devices, slot_count), ('gx', 'yz'), spli...]
    all_to_all x3 -> x0, waiting for transfers between devices: 10.1 us -> none  [the longest x1 6.14 us: local(): lax.all_to_all(answer, ('gx', 'yz'), split_axis=1, concat_axis=1, tiled=T...]
    ppermute x4 -> x0, starting transfers between devices: 6.57 us -> none  [the longest x2 5.88 us: extended(): lax.ppermute(lax.slice_in_dim(block, 0, width, axis=dim), axis, backward)]
    dynamic_slice x16 -> x0, local copies, waits for them, and re-layouts: 6.25 us -> none  [local(): lax.map(wall_plane, plane_ids)]
    unnamed x19 -> x0, other arithmetic: 2.97 us -> none
    ppermute x4 -> x0, waiting for transfers between devices: 2.6 us -> none  [the longest x2 2.6 us: extended(): lax.ppermute(lax.slice_in_dim(block, block.shape[dim] - width, None, axis...]
  transfers between devices with their start and end apart: 7 -> 0, of which waited for: 4 -> 0; matrix products, arithmetic and copies ran while one was open for 12% -> 0% of each run, Pallas kernels for 0% -> 0%
where the time goes in v1:
time: 35 us; the launch traced here: 34.8 us
  Pallas kernels  30.9 us (88%)
  local copies, waits for them, and re-layouts  3.27 us (9%)
  between operations  0.65 us (2%)
    pallas_call x1, Pallas kernels, local(): pl.pallas_call(functools.partial(kernel, count_x, count_y, slot), out_sha...  30.9 us
    unnamed x7, local copies, waits for them, and re-layouts  3.27 us

profile of v1, /device:TPU:0, one launch (start us, length us, event | category | flops | bytes accessed | tf_op | source)
XLA Modules:
  0.0 34.8 jit_solution(5973943993209887358)
XLA Ops:
  0.6 30.9 %step.1 = (f32[19,8,8,128]{3,2,1,0:T(8,128)}, f32[3,512]{1,0:T(4,128)}, f32[3,512]{1,0:T(4,128)}) custom-call(f32[19,8,8,128]{3,2,1,0:T(8,128)} %pops.1, s32[8,8,128]{2,1,0:T(8,128)} %cells.1, s32[8,1,128]{2,1,0:T(1,128)} %bitcast.3, s32[2,1024]{1,0:T(2,128)} %pairs.1, f32[3,512]{1,0:T(4,128)} %position.1, f32[3,512]{1,0:T(4,128)} %velocity.1, ...), custom_call_target="tpu_custom_call" | custom-call | tf_op jit(solution)/shard_map/step/pallas_call | solution.py:488
  31.5 0.0 copy-start.1
  31.5 2.0 %copy.14 = f32[19,8,8,128]{3,2,1,0:T(8,128)} copy(f32[19,8,8,128]{3,2,1,0:T(8,128)} %get-tuple-element.6) | data formatting | bytes 1245184
  33.5 0.0 copy-done.1
  33.5 0.0 copy-start
  33.5 0.6 %copy.15 = f32[3,512]{1,0:T(4,128)} copy(f32[3,512]{1,0:T(4,128)S(1)} %copy-done.1) | data formatting | bytes 12288
  34.1 0.1 copy-done
  34.2 0.6 %copy.16 = f32[3,512]{1,0:T(4,128)} copy(f32[3,512]{1,0:T(4,128)S(1)} %copy-done) | data formatting | bytes 12288
Async XLA Ops:
  31.5 2.0 %copy-start.1 = (f32[3,512]{1,0:T(4,128)S(1)}, f32[3,512]{1,0:T(4,128)}, u32[]{:S(2)}) copy-start(f32[3,512]{1,0:T(4,128)} %get-tuple-element.7) | copy-start | bytes 18436
  33.5 0.7 %copy-start = (f32[3,512]{1,0:T(4,128)S(1)}, f32[3,512]{1,0:T(4,128)}, u32[]{:S(2)}) copy-start(f32[3,512]{1,0:T(4,128)} %get-tuple-element.8) | copy-start | bytes 18436

commit v2 on v1

--- a/solution.py
+++ b/solution.py
@@ -66,6 +66,10 @@
 def lookup(row, lanes):
     table = jnp.broadcast_to(row, lanes.shape)
     return jnp.take_along_axis(table, lanes, axis=1, mode="promise_in_bounds")
+
+
+def split(ids):
+    return lax.shift_right_arithmetic(ids, 7), jnp.bitwise_and(ids, LANE - 1)
 
 
 def lane_roll(value, shift):
@@ -121,6 +125,15 @@
     count_x,
     count_y,
     slot,
+    pops_in,
+    cells_in,
+    near_in,
+    pairs_in,
+    position_in,
+    velocity_in,
+    radius_in,
+    out_pops,
+    out_force,
     pops,
     cells,
     near,
@@ -128,10 +141,6 @@
     position,
     velocity,
     radius,
-    mass,
-    out_pops,
-    out_vel,
-    out_pos,
     asked,
     reply,
     known,
@@ -148,6 +157,7 @@
     recv_sems,
     halo_send,
     halo_recv,
+    load_sems,
 ):
     devices = count_x * count_y
     groups = devices // SUB
@@ -161,43 +171,61 @@
     sub = lax.broadcasted_iota(jnp.int32, (SUB, LANE), 0)
     lane = lax.broadcasted_iota(jnp.int32, (SUB, LANE), 1)
 
-    def peer_of(step):
-        peer = lax.rem(me + step, devices)
-        return peer, (peer // count_y, lax.rem(peer, count_y))
+    offsets = [
+        (step_x, step_y)
+        for step_x in sorted(range(count_x), key=lambda step: abs(2 * step - count_x))
+        for step_y in reversed(range(count_y))
+        if step_x or step_y
+    ]
+    line_x = [lax.rem(at_x + step, count_x) for step in range(count_x)]
+    line_y = [lax.rem(at_y + step, count_y) for step in range(count_y)]
 
     barrier = pltpu.get_barrier_semaphore()
-
-    def greet(step, carry):
-        peer, where = peer_of(step)
+    for step_x, step_y in offsets:
         pl.semaphore_signal(
-            barrier, inc=1, device_id=where, device_id_type=pl.DeviceIdType.MESH
+            barrier,
+            inc=1,
+            device_id=(line_x[step_x], line_y[step_y]),
+            device_id_type=pl.DeviceIdType.MESH,
         )
-        return carry
-
-    lax.fori_loop(1, devices, greet, 0)
+    loads = []
+    for place, (source, target) in enumerate(
+        (
+            (near_in, near),
+            (velocity_in, velocity),
+            (position_in, position),
+            (radius_in, radius),
+            (pops_in, pops),
+            (cells_in, cells),
+            (pairs_in, pairs),
+        )
+    ):
+        load = pltpu.make_async_copy(source, target, load_sems.at[place])
+        load.start()
+        loads.append(load)
+    loads[0].wait()
     asked[pl.ds(me, 1)] = near[pl.ds(me // per_row, 1)]
     pl.semaphore_wait(barrier, devices - 1)
 
     def everyone(source_of, target, which):
-        def start(step, carry):
-            peer, where = peer_of(step)
+        for step_x, step_y in offsets:
+            to_x, to_y = line_x[step_x], line_y[step_y]
             pltpu.make_async_remote_copy(
-                src_ref=source_of(peer),
+                src_ref=source_of(to_x * count_y + to_y),
                 dst_ref=target.at[pl.ds(me, 1)],
                 send_sem=send_sems.at[which],
                 recv_sem=recv_sems.at[which],
-                device_id=where,
+                device_id=(to_x, to_y),
                 device_id_type=pl.DeviceIdType.MESH,
             ).start()
-            return carry
-
-        lax.fori_loop(1, devices, start, 0)
 
     def arrived(target, sems, which):
         part = target.at[pl.ds(0, devices - 1)]
         pltpu.make_async_copy(part, part, sems.at[which]).wait()
 
     everyone(lambda peer: near.at[pl.ds(peer // per_row, 1)], asked, 0)
+    for load in loads[1:]:
+        load.wait()
 
     def collide(x, carry):
         values = [pops[i, x] for i in range(19)]
@@ -242,8 +270,9 @@
 
     arrived(asked, recv_sems, 0)
     quarter = lax.rem(me, per_row)
-    field = lane // slot
-    within = lane - field * slot
+    slot_bits = slot.bit_length() - 1
+    field = lax.shift_right_logical(lane, slot_bits)
+    within = jnp.bitwise_and(lane, slot - 1)
     wanted = []
     for q in range(groups):
         ask = asked[q * SUB : (q + 1) * SUB, 0, :]
@@ -252,8 +281,7 @@
         )
         wanted.append(row)
         safe = jnp.maximum(row, 0)
-        bank = safe // LANE
-        spot = safe - bank * LANE
+        bank, spot = split(safe)
         vel_row = jnp.zeros((SUB, LANE), jnp.float32)
         pos_row = jnp.zeros((SUB, LANE), jnp.float32)
         for h in range(banks):
@@ -268,7 +296,7 @@
         reply[q * SUB : (q + 1) * SUB, 1, :] = pos_row
     everyone(lambda peer: reply.at[pl.ds(peer, 1)], known, 1)
 
-    part_of_lane = lane // slot
+    part_of_lane = field
 
     def to_table(read, compo):
         value = jnp.zeros((SUB, LANE), jnp.float32)
@@ -280,9 +308,7 @@
     wanted_table = jnp.zeros((SUB, LANE), jnp.int32)
     for q in range(groups):
         wanted_table = jnp.where(part_of_lane == q, lane_roll(wanted[q], q * slot), wanted_table)
-    wanted_bank = wanted_table // LANE
-    wanted_bank = jnp.where(wanted_table < 0, SUB, wanted_bank)
-    wanted_spot = jnp.bitwise_and(wanted_table, LANE - 1)
+    wanted_bank, wanted_spot = split(wanted_table)
 
     arrived(known, recv_sems, 1)
     known[pl.ds(me, 1)] = reply[pl.ds(me, 1)]
@@ -292,10 +318,10 @@
     vel_rows = [[part[r : r + 1] for r in range(SUB)] for part in vel_table]
 
     def entry(ids):
-        owner = ids // slot
-        inner = ids - owner * slot
-        row = jnp.bitwise_and(owner, SUB - 1)
-        return row, (owner // SUB) * slot + inner
+        row = jnp.bitwise_and(lax.shift_right_logical(ids, slot_bits), SUB - 1)
+        part = lax.shift_right_logical(ids, slot_bits + 3)
+        inner = jnp.bitwise_and(ids, slot - 1)
+        return row, jnp.bitwise_and(lax.shift_left(part, slot_bits) + inner, LANE - 1)
 
     def from_table(rows_of, row, spot):
         value = jnp.zeros((SUB, LANE), jnp.float32)
@@ -306,7 +332,7 @@
     def fill_walls(x, carry):
         ids = cells[x]
         solid = ids >= 0
-        row, spot = entry(jnp.maximum(ids, 0))
+        row, spot = entry(ids)
         speeds = [from_table(rows_of, row, spot) for rows_of in vel_rows]
         for compo in range(3):
             wall[compo, x] = speeds[compo]
@@ -360,8 +386,7 @@
         pair_ids[0, y : y + 1] = pairs[0:1, y * LANE : (y + 1) * LANE]
         pair_ids[1, y : y + 1] = pairs[1:2, y * LANE : (y + 1) * LANE]
     first = pair_ids[0]
-    first_bank = first // LANE
-    first_spot = first - first_bank * LANE
+    first_bank, first_spot = split(first)
 
     def from_owned(ref, compo):
         value = jnp.zeros((SUB, LANE), jnp.float32)
@@ -434,7 +459,7 @@
                 elif shift[compo] < 0:
                     force[compo] = force[compo] - link
         force = [jnp.where(solid, part, 0.0) for part in force]
-        where = entry(jnp.maximum(cells[x], 0))
+        where = entry(cells[x])
         return total + sums_by_entry(force, *where)
 
     slot_force = lax.fori_loop(0, width, stream, jnp.zeros((32, LANE), jnp.float32))
@@ -459,9 +484,7 @@
         for h in range(banks):
             span = slice(h * LANE, (h + 1) * LANE)
             line = compo * SUB + h
-            speed = velocity[compo : compo + 1, span] + force[line : line + 1] / mass[0:1, span]
-            out_vel[compo : compo + 1, span] = speed
-            out_pos[compo : compo + 1, span] = position[compo : compo + 1, span] + speed
+            out_force[compo : compo + 1, span] = force[line : line + 1]
     arrived(sent_force, send_sems, 2)
 
 
@@ -485,16 +508,24 @@
     near_lines = near_rows.reshape(near_count // LANE, 1, LANE)
     whole = pl.BlockSpec(memory_space=pltpu.VMEM)
     f32 = jnp.float32
-    return pl.pallas_call(
+    assert slot & (slot - 1) == 0 and near_count == SUB * LANE
+    radius_line = grain_radius.reshape(1, owned)
+    read, force = pl.pallas_call(
         functools.partial(kernel, count_x, count_y, slot),
         out_shape=(
-            jax.ShapeDtypeStruct(populations.shape, f32),
+            pltpu.VMEM(populations.shape, f32),
             jax.ShapeDtypeStruct(grain_velocity.shape, f32),
-            jax.ShapeDtypeStruct(grain_position.shape, f32),
         ),
-        in_specs=[whole] * 8,
-        out_specs=(whole,) * 3,
+        in_specs=[pl.BlockSpec(memory_space=pltpu.HBM)] * 7,
+        out_specs=(whole,) * 2,
         scratch_shapes=[
+            pltpu.VMEM(populations.shape, f32),
+            pltpu.VMEM(cell_grain.shape, jnp.int32),
+            pltpu.VMEM(near_lines.shape, jnp.int32),
+            pltpu.VMEM(contact_pairs.shape, jnp.int32),
+            pltpu.VMEM(grain_position.shape, f32),
+            pltpu.VMEM(grain_velocity.shape, f32),
+            pltpu.VMEM(radius_line.shape, f32),
             pltpu.VMEM((devices, 1, LANE), jnp.int32),
             pltpu.VMEM((devices, 2, LANE), f32),
             pltpu.VMEM((devices, 2, LANE), f32),
@@ -511,19 +542,28 @@
             pltpu.SemaphoreType.DMA((3,)),
             pltpu.SemaphoreType.DMA((8,)),
             pltpu.SemaphoreType.DMA((8,)),
+            pltpu.SemaphoreType.DMA((7,)),
         ],
-        compiler_params=pltpu.CompilerParams(collective_id=0, has_side_effects=True),
+        compiler_params=pltpu.CompilerParams(
+            collective_id=0, has_side_effects=True, vmem_limit_bytes=24 << 20
+        ),
         name="step",
     )(
-        populations,
-        cell_grain,
-        near_lines,
-        contact_pairs,
-        grain_position,
-        grain_velocity,
-        grain_radius.reshape(1, owned),
-        grain_mass.reshape(1, owned),
+        *(
+            pltpu.with_memory_space_constraint(array, pltpu.HBM)
+            for array in (
+                populations,
+                cell_grain,
+                near_lines,
+                contact_pairs,
+                grain_position,
+                grain_velocity,
+                radius_line,
+            )
+        )
     )
+    velocity_next = grain_velocity + force / grain_mass[None]
+    return read, velocity_next, grain_position + velocity_next
 
 
 def solution(mesh):

time: 35 us -> 31.5 us (0.900)
  local copies, waits for them, and re-layouts: 3.27 us -> 0.85 us
  Pallas kernels: 30.9 us -> 29.1 us
  other arithmetic: 0 us -> 0.61 us
    unnamed x7, local copies, waits for them, and re-layouts: 3.27 us -> 0.85 us
    pallas_call x1, Pallas kernels: 30.9 us -> 29.1 us  [local(): pl.pallas_call(functools.partial(kernel, count_x, count_y, slot), out_sha...]
    add x0 -> x1, other arithmetic: none -> 0.61 us  [local(): return (read, velocity_next, grain_position + velocity_next)]
where the time goes in v2:
time: 31.5 us; the launch traced here: 31.3 us
  Pallas kernels  29.1 us (92%)
  local copies, waits for them, and re-layouts  0.85 us (3%)
  between operations  0.67 us (2%)
  other arithmetic  0.61 us (2%)
    pallas_call x1, Pallas kernels, local(): pl.pallas_call(functools.partial(kernel, count_x, count_y, slot), out_sha...  29.1 us
    unnamed x7, local copies, waits for them, and re-layouts  0.85 us

profile of v2, /device:TPU:0, one launch (start us, length us, event | category | flops | bytes accessed | tf_op | source)
XLA Modules:
  0.0 31.3 jit_solution(15437205777577817258)
XLA Ops:
  0.6 29.1 %step.1 = (f32[19,8,8,128]{3,2,1,0:T(8,128)S(1)}, f32[3,512]{1,0:T(4,128)S(1)}) custom-call(f32[19,8,8,128]{3,2,1,0:T(8,128)} %pops_in.1, s32[8,8,128]{2,1,0:T(8,128)} %cells_in.1, s32[8,1,128]{2,1,0:T(1,128)} %bitcast.2, s32[2,1024]{1,0:T(2,128)} %pairs_in.1, f32[3,512]{1,0:T(4,128)} %position_in.1, f32[3,512]{1,0:T(4,128)} %velocity_in.1, f32[1,512]{1,0:T(1,128)} %bitcast.3), custom_call_target="tpu_custom_call" | custom-call | tf_op jit(solution)/shard_map/step/pallas_call | solution.py:513
  29.8 0.0 copy-start
  29.8 0.0 copy-start.1
  29.8 0.0 copy-start.2
  29.8 0.8 %copy.12 = f32[19,8,8,128]{3,2,1,0:T(8,128)} copy(f32[19,8,8,128]{3,2,1,0:T(8,128)S(1)} %get-tuple-element.9) | data formatting | bytes 1245184
  30.7 0.0 copy-done
  30.7 0.0 copy-done.1
  30.7 0.0 copy-done.2
  30.7 0.6 %fusion = (f32[3,512]{1,0:T(4,128)}, f32[3,512]{1,0:T(4,128)}) fusion(f32[3,512]{1,0:T(4,128)S(1)} %copy-done, f32[3,512]{1,0:T(4,128)S(1)} %copy-done.1, f32[3,512]{1,0:T(4,128)S(1)} %get-tuple-element.6, f32[512]{0:T(512)S(1)} %copy-done.2), kind=kLoop, calls=%fused_computation.1 | loop fusion | flops 4608 | bytes 32768 | tf_op jit(solution)/shard_map/add | solution.py:566
Async XLA Ops:
  29.8 0.9 %copy-start = (f32[3,512]{1,0:T(4,128)S(1)}, f32[3,512]{1,0:T(4,128)}, u32[]{:S(2)}) copy-start(f32[3,512]{1,0:T(4,128)} %position_in.1) | copy-start | bytes 18436
  29.8 0.9 %copy-start.1 = (f32[3,512]{1,0:T(4,128)S(1)}, f32[3,512]{1,0:T(4,128)}, u32[]{:S(2)}) copy-start(f32[3,512]{1,0:T(4,128)} %velocity_in.1) | copy-start | bytes 18436
  29.8 0.8 %copy-start.2 = (f32[512]{0:T(512)S(1)}, f32[512]{0:T(512)}, u32[]{:S(2)}) copy-start(f32[512]{0:T(512)} %param.15) | copy-start | bytes 6148

commit v3 on v2

--- a/solution.py
+++ b/solution.py
@@ -141,6 +141,9 @@
     position,
     velocity,
     radius,
+    vel_lines,
+    all_vel,
+    measure_vel,
     asked,
     reply,
     known,
@@ -203,16 +206,24 @@
         load = pltpu.make_async_copy(source, target, load_sems.at[place])
         load.start()
         loads.append(load)
+    my_line = me // per_row
+    my_place = lax.rem(me, per_row)
+    loads[1].wait()
+    for compo in range(3):
+        for h in range(banks):
+            line = velocity[compo : compo + 1, h * LANE : (h + 1) * LANE]
+            vel_lines[compo * banks + h] = line
+            all_vel[my_place, compo * banks + h, my_line] = line
     loads[0].wait()
     asked[pl.ds(me, 1)] = near[pl.ds(me // per_row, 1)]
     pl.semaphore_wait(barrier, devices - 1)
 
-    def everyone(source_of, target, which):
+    def everyone(source_of, target_at_me, which):
         for step_x, step_y in offsets:
             to_x, to_y = line_x[step_x], line_y[step_y]
             pltpu.make_async_remote_copy(
                 src_ref=source_of(to_x * count_y + to_y),
-                dst_ref=target.at[pl.ds(me, 1)],
+                dst_ref=target_at_me,
                 send_sem=send_sems.at[which],
                 recv_sem=recv_sems.at[which],
                 device_id=(to_x, to_y),
@@ -220,11 +231,12 @@
             ).start()
 
     def arrived(target, sems, which):
-        part = target.at[pl.ds(0, devices - 1)]
+        part = target if target is measure_vel else target.at[pl.ds(0, devices - 1)]
         pltpu.make_async_copy(part, part, sems.at[which]).wait()
 
-    everyone(lambda peer: near.at[pl.ds(peer // per_row, 1)], asked, 0)
-    for load in loads[1:]:
+    everyone(lambda peer: vel_lines, all_vel.at[my_place, :, my_line], 3)
+    everyone(lambda peer: near.at[peer // per_row], asked.at[me], 0)
+    for load in loads[2:]:
         load.wait()
 
     def collide(x, carry):
@@ -268,60 +280,23 @@
 
     lax.fori_loop(0, width, collide, 0)
 
-    arrived(asked, recv_sems, 0)
-    quarter = lax.rem(me, per_row)
     slot_bits = slot.bit_length() - 1
     field = lax.shift_right_logical(lane, slot_bits)
-    within = jnp.bitwise_and(lane, slot - 1)
-    wanted = []
-    for q in range(groups):
-        ask = asked[q * SUB : (q + 1) * SUB, 0, :]
-        row = jnp.take_along_axis(
-            ask, within + quarter * slot, axis=1, mode="promise_in_bounds"
-        )
-        wanted.append(row)
-        safe = jnp.maximum(row, 0)
-        bank, spot = split(safe)
-        vel_row = jnp.zeros((SUB, LANE), jnp.float32)
-        pos_row = jnp.zeros((SUB, LANE), jnp.float32)
+    near_bank, near_spot = split(
+        jnp.concatenate([near[line] for line in range(SUB)], axis=0)
+    )
+    arrived(measure_vel, recv_sems, 3)
+    vel_table = [jnp.zeros((SUB, LANE), jnp.float32) for compo in range(3)]
+    for place in range(per_row):
         for h in range(banks):
-            span = slice(h * LANE, (h + 1) * LANE)
+            mine = (field == place) & (near_bank == h)
             for compo in range(3):
-                mine = (bank == h) & (field == compo)
-                vel_row = jnp.where(mine, lookup(velocity[compo : compo + 1, span], spot), vel_row)
-                pos_row = jnp.where(mine, lookup(position[compo : compo + 1, span], spot), pos_row)
-            mine = (bank == h) & (field == 3)
-            pos_row = jnp.where(mine, lookup(radius[0:1, span], spot), pos_row)
-        reply[q * SUB : (q + 1) * SUB, 0, :] = vel_row
-        reply[q * SUB : (q + 1) * SUB, 1, :] = pos_row
-    everyone(lambda peer: reply.at[pl.ds(peer, 1)], known, 1)
-
-    part_of_lane = field
-
-    def to_table(read, compo):
-        value = jnp.zeros((SUB, LANE), jnp.float32)
-        for q in range(groups):
-            moved = lane_roll(read(q), (q - compo) * slot)
-            value = jnp.where(part_of_lane == q, moved, value)
-        return value
-
-    wanted_table = jnp.zeros((SUB, LANE), jnp.int32)
-    for q in range(groups):
-        wanted_table = jnp.where(part_of_lane == q, lane_roll(wanted[q], q * slot), wanted_table)
-    wanted_bank, wanted_spot = split(wanted_table)
-
-    arrived(known, recv_sems, 1)
-    known[pl.ds(me, 1)] = reply[pl.ds(me, 1)]
-    vel_table = [
-        to_table(lambda q: known[q * SUB : (q + 1) * SUB, 0, :], compo) for compo in range(3)
-    ]
+                lines = all_vel[place, compo * banks + h, :, 0, :]
+                part = jnp.take_along_axis(
+                    lines, near_spot, axis=1, mode="promise_in_bounds"
+                )
+                vel_table[compo] = jnp.where(mine, part, vel_table[compo])
     vel_rows = [[part[r : r + 1] for r in range(SUB)] for part in vel_table]
-
-    def entry(ids):
-        row = jnp.bitwise_and(lax.shift_right_logical(ids, slot_bits), SUB - 1)
-        part = lax.shift_right_logical(ids, slot_bits + 3)
-        inner = jnp.bitwise_and(ids, slot - 1)
-        return row, jnp.bitwise_and(lax.shift_left(part, slot_bits) + inner, LANE - 1)
 
     def from_table(rows_of, row, spot):
         value = jnp.zeros((SUB, LANE), jnp.float32)
@@ -332,7 +307,7 @@
     def fill_walls(x, carry):
         ids = cells[x]
         solid = ids >= 0
-        row, spot = entry(ids)
+        row, spot = split(ids)
         speeds = [from_table(rows_of, row, spot) for rows_of in vel_rows]
         for compo in range(3):
             wall[compo, x] = speeds[compo]
@@ -382,36 +357,31 @@
         copy.start()
         copies.append(copy)
 
-    for y in range(SUB):
-        pair_ids[0, y : y + 1] = pairs[0:1, y * LANE : (y + 1) * LANE]
-        pair_ids[1, y : y + 1] = pairs[1:2, y * LANE : (y + 1) * LANE]
-    first = pair_ids[0]
-    first_bank, first_spot = split(first)
-
-    def from_owned(ref, compo):
-        value = jnp.zeros((SUB, LANE), jnp.float32)
+    arrived(asked, recv_sems, 0)
+    quarter = my_place
+    within = jnp.bitwise_and(lane, slot - 1)
+    wanted = []
+    for q in range(groups):
+        ask = asked[q * SUB : (q + 1) * SUB, 0, :]
+        row = jnp.take_along_axis(
+            ask, within + quarter * slot, axis=1, mode="promise_in_bounds"
+        )
+        wanted.append(row)
+        bank, spot = split(jnp.maximum(row, 0))
+        pos_row = jnp.zeros((SUB, LANE), jnp.float32)
         for h in range(banks):
-            part = lookup(ref[compo : compo + 1, h * LANE : (h + 1) * LANE], first_spot)
-            value = jnp.where(first_bank == h, part, value)
-        return value
-
-    row, spot = entry(pair_ids[1])
-
-    def from_known(field_table):
-        return from_table([field_table[r : r + 1] for r in range(SUB)], row, spot)
-
-    pos_table = [
-        to_table(lambda q: known[q * SUB : (q + 1) * SUB, 1, :], compo) for compo in range(4)
-    ]
-    push = contact_push(
-        [from_owned(position, compo) for compo in range(3)],
-        [from_owned(velocity, compo) for compo in range(3)],
-        from_owned(radius, 0),
-        [from_known(pos_table[compo]) for compo in range(3)],
-        [from_known(vel_table[compo]) for compo in range(3)],
-        from_known(pos_table[3]),
-    )
-    contact = sums_by_entry(push, first_bank, first_spot)
+            span = slice(h * LANE, (h + 1) * LANE)
+            for compo in range(4):
+                source = radius[0:1, span] if compo == 3 else position[compo : compo + 1, span]
+                mine = (bank == h) & (field == compo)
+                pos_row = jnp.where(mine, lookup(source, spot), pos_row)
+        reply[q * SUB : (q + 1) * SUB, 0, :] = pos_row
+    everyone(lambda peer: reply.at[peer], known.at[my_place, my_line], 1)
+
+    wanted_table = jnp.zeros((SUB, LANE), jnp.int32)
+    for q in range(groups):
+        wanted_table = jnp.where(field == q, lane_roll(wanted[q], q * slot), wanted_table)
+    wanted_bank, wanted_spot = split(wanted_table)
 
     for copy in copies:
         copy.wait()
@@ -459,25 +429,72 @@
                 elif shift[compo] < 0:
                     force[compo] = force[compo] - link
         force = [jnp.where(solid, part, 0.0) for part in force]
-        where = entry(cells[x])
+        where = split(cells[x])
         return total + sums_by_entry(force, *where)
 
     slot_force = lax.fori_loop(0, width, stream, jnp.zeros((32, LANE), jnp.float32))
 
-    for q in range(groups):
+    for place in range(per_row):
         value = jnp.zeros((SUB, LANE), jnp.float32)
         for compo in range(3):
-            part = lane_roll(slot_force[compo * SUB : (compo + 1) * SUB], (compo - q) * slot)
+            part = lane_roll(slot_force[compo * SUB : (compo + 1) * SUB], (compo - place) * slot)
             value = jnp.where(field == compo, part, value)
-        sent_force[q * SUB : (q + 1) * SUB, 0, :] = value
-    everyone(lambda peer: sent_force.at[pl.ds(peer, 1)], got_force, 2)
+        sent_force[place, :, 0, :] = value
+    everyone(
+        lambda peer: sent_force.at[lax.rem(peer, per_row), peer // per_row],
+        got_force.at[me],
+        2,
+    )
+
+    for y in range(SUB):
+        pair_ids[0, y : y + 1] = pairs[0:1, y * LANE : (y + 1) * LANE]
+        pair_ids[1, y : y + 1] = pairs[1:2, y * LANE : (y + 1) * LANE]
+    first = pair_ids[0]
+    first_bank, first_spot = split(first)
+
+    def from_owned(ref, compo):
+        value = jnp.zeros((SUB, LANE), jnp.float32)
+        for h in range(banks):
+            part = lookup(ref[compo : compo + 1, h * LANE : (h + 1) * LANE], first_spot)
+            value = jnp.where(first_bank == h, part, value)
+        return value
+
+    row, spot = split(pair_ids[1])
+
+    def from_known(field_table):
+        return from_table([field_table[r : r + 1] for r in range(SUB)], row, spot)
+
+    arrived(got_force, recv_sems, 1)
+    known[my_place, my_line] = reply[me]
+    pos_table = []
+    for compo in range(4):
+        value = jnp.zeros((SUB, LANE), jnp.float32)
+        for place in range(per_row):
+            moved_lanes = lane_roll(known[place, :, 0, :], (place - compo) * slot)
+            value = jnp.where(field == place, moved_lanes, value)
+        pos_table.append(value)
+    push = contact_push(
+        [from_owned(position, compo) for compo in range(3)],
+        [from_owned(velocity, compo) for compo in range(3)],
+        from_owned(radius, 0),
+        [from_known(pos_table[compo]) for compo in range(3)],
+        [from_known(vel_table[compo]) for compo in range(3)],
+        from_known(pos_table[3]),
+    )
+    contact = sums_by_entry(push, first_bank, first_spot)
+
+    arrived(measure_vel, send_sems, 3)
     arrived(asked, send_sems, 0)
     arrived(reply, send_sems, 1)
     arrived(got_force, recv_sems, 2)
-    got_force[pl.ds(me, 1)] = sent_force[pl.ds(me, 1)]
-    gained = [
-        to_table(lambda q: got_force[q * SUB : (q + 1) * SUB, 0, :], compo) for compo in range(3)
-    ]
+    got_force[me] = sent_force[my_place, my_line]
+    gained = []
+    for compo in range(3):
+        value = jnp.zeros((SUB, LANE), jnp.float32)
+        for q in range(groups):
+            part = got_force[q * SUB : (q + 1) * SUB, 0, :]
+            value = jnp.where(field == q, lane_roll(part, (q - compo) * slot), value)
+        gained.append(value)
     fluid_force = sums_by_entry(gained, wanted_bank, wanted_spot)
     force = fluid_force + contact
     for compo in range(3):
@@ -485,7 +502,7 @@
             span = slice(h * LANE, (h + 1) * LANE)
             line = compo * SUB + h
             out_force[compo : compo + 1, span] = force[line : line + 1]
-    arrived(sent_force, send_sems, 2)
+    arrived(got_force, send_sems, 2)
 
 
 def local(
@@ -509,6 +526,8 @@
     whole = pl.BlockSpec(memory_space=pltpu.VMEM)
     f32 = jnp.float32
     assert slot & (slot - 1) == 0 and near_count == SUB * LANE
+    lines = 3 * owned // LANE
+    per_row = LANE // slot
     radius_line = grain_radius.reshape(1, owned)
     read, force = pl.pallas_call(
         functools.partial(kernel, count_x, count_y, slot),
@@ -526,10 +545,13 @@
             pltpu.VMEM(grain_position.shape, f32),
             pltpu.VMEM(grain_velocity.shape, f32),
             pltpu.VMEM(radius_line.shape, f32),
+            pltpu.VMEM((lines, 1, LANE), f32),
+            pltpu.VMEM((per_row, lines, SUB, 1, LANE), f32),
+            pltpu.VMEM(((devices - 1) * lines, 1, LANE), f32),
             pltpu.VMEM((devices, 1, LANE), jnp.int32),
-            pltpu.VMEM((devices, 2, LANE), f32),
-            pltpu.VMEM((devices, 2, LANE), f32),
             pltpu.VMEM((devices, 1, LANE), f32),
+            pltpu.VMEM((per_row, SUB, 1, LANE), f32),
+            pltpu.VMEM((per_row, SUB, 1, LANE), f32),
             pltpu.VMEM((devices, 1, LANE), f32),
             pltpu.VMEM((CHANNELS, width + 2, SUB, LANE), f32),
             pltpu.VMEM((3, width, SUB, LANE), f32),
@@ -538,8 +560,8 @@
             pltpu.VMEM((FACE, width + 2, 1, LANE), f32),
             pltpu.VMEM((FACE, width + 2, 1, LANE), f32),
             pltpu.VMEM((2, SUB, LANE), jnp.int32),
-            pltpu.SemaphoreType.DMA((3,)),
-            pltpu.SemaphoreType.DMA((3,)),
+            pltpu.SemaphoreType.DMA((4,)),
+            pltpu.SemaphoreType.DMA((4,)),
             pltpu.SemaphoreType.DMA((8,)),
             pltpu.SemaphoreType.DMA((8,)),
             pltpu.SemaphoreType.DMA((7,)),

time: 31.5 us -> 27.4 us (0.87)
  Pallas kernels: 29.1 us -> 25.1 us
    pallas_call x1, Pallas kernels: 29.1 us -> 25.1 us  [local(): pl.pallas_call(functools.partial(kernel, count_x, count_y, slot), out_sha...]
where the time goes in v3:
time: 27.4 us; the launch traced here: 27.2 us
  Pallas kernels  25.1 us (92%)
  local copies, waits for them, and re-layouts  0.85 us (3%)
  between operations  0.67 us (2%)
  other arithmetic  0.61 us (2%)
    pallas_call x1, Pallas kernels, local(): pl.pallas_call(functools.partial(kernel, count_x, count_y, slot), out_sha...  25.1 us
    unnamed x7, local copies, waits for them, and re-layouts  0.85 us
    add x1, other arithmetic, local(): return (read, velocity_next, grain_position + velocity_next)  0.61 us

profile of v3, /device:TPU:0, one launch (start us, length us, event | category | flops | bytes accessed | tf_op | source)
XLA Modules:
  0.0 27.2 jit_solution(6456379561487489087)
XLA Ops:
  0.6 25.1 %step.1 = (f32[19,8,8,128]{3,2,1,0:T(8,128)S(1)}, f32[3,512]{1,0:T(4,128)S(1)}) custom-call(f32[19,8,8,128]{3,2,1,0:T(8,128)} %pops_in.1, s32[8,8,128]{2,1,0:T(8,128)} %cells_in.1, s32[8,1,128]{2,1,0:T(1,128)} %bitcast.2, s32[2,1024]{1,0:T(2,128)} %pairs_in.1, f32[3,512]{1,0:T(4,128)} %position_in.1, f32[3,512]{1,0:T(4,128)} %velocity_in.1, f32[1,512]{1,0:T(1,128)} %bitcast.3), custom_call_target="tpu_custom_call" | custom-call | tf_op jit(solution)/shard_map/step/pallas_call | solution.py:532
  25.7 0.0 copy-start
  25.8 0.0 copy-start.1
  25.8 0.0 copy-start.2
  25.8 0.8 %copy.12 = f32[19,8,8,128]{3,2,1,0:T(8,128)} copy(f32[19,8,8,128]{3,2,1,0:T(8,128)S(1)} %get-tuple-element.9) | data formatting | bytes 1245184
  26.6 0.0 copy-done
  26.6 0.0 copy-done.1
  26.6 0.0 copy-done.2
  26.6 0.6 %fusion = (f32[3,512]{1,0:T(4,128)}, f32[3,512]{1,0:T(4,128)}) fusion(f32[3,512]{1,0:T(4,128)S(1)} %copy-done, f32[3,512]{1,0:T(4,128)S(1)} %copy-done.1, f32[3,512]{1,0:T(4,128)S(1)} %get-tuple-element.6, f32[512]{0:T(512)S(1)} %copy-done.2), kind=kLoop, calls=%fused_computation.1 | loop fusion | flops 4608 | bytes 32768 | tf_op jit(solution)/shard_map/add | solution.py:588
Async XLA Ops:
  25.7 0.9 %copy-start = (f32[3,512]{1,0:T(4,128)S(1)}, f32[3,512]{1,0:T(4,128)}, u32[]{:S(2)}) copy-start(f32[3,512]{1,0:T(4,128)} %position_in.1) | copy-start | bytes 18436
  25.8 0.9 %copy-start.1 = (f32[3,512]{1,0:T(4,128)S(1)}, f32[3,512]{1,0:T(4,128)}, u32[]{:S(2)}) copy-start(f32[3,512]{1,0:T(4,128)} %velocity_in.1) | copy-start | bytes 18436
  25.8 0.8 %copy-start.2 = (f32[512]{0:T(512)S(1)}, f32[512]{0:T(512)}, u32[]{:S(2)}) copy-start(f32[512]{0:T(512)} %param.15) | copy-start | bytes 6148

commit v4 on v3

--- a/solution.py
+++ b/solution.py
@@ -327,7 +327,7 @@
         low_src[4, pl.ds(x, 1)] = rho[0:1][None]
         return carry
 
-    lax.fori_loop(0, width, fill_walls, 0)
+    lax.fori_loop(0, width, fill_walls, 0, unroll=4)
 
     right = lax.rem(at_x + 1, count_x)
     left = lax.rem(at_x + count_x - 1, count_x)
@@ -432,7 +432,7 @@
         where = split(cells[x])
         return total + sums_by_entry(force, *where)
 
-    slot_force = lax.fori_loop(0, width, stream, jnp.zeros((32, LANE), jnp.float32))
+    slot_force = lax.fori_loop(0, width, stream, jnp.zeros((32, LANE), jnp.float32), unroll=4)
 
     for place in range(per_row):
         value = jnp.zeros((SUB, LANE), jnp.float32)

time: 27.4 us -> 25.9 us (0.945)
  Pallas kernels: 25.1 us -> 23.6 us
    pallas_call x1, Pallas kernels: 25.1 us -> 23.6 us  [local(): pl.pallas_call(functools.partial(kernel, count_x, count_y, slot), out_sha...]
where the time goes in v4:
time: 25.9 us; the launch traced here: 25.7 us
  Pallas kernels  23.6 us (91%)
  local copies, waits for them, and re-layouts  0.85 us (3%)
  between operations  0.67 us (3%)
  other arithmetic  0.61 us (2%)
    pallas_call x1, Pallas kernels, local(): pl.pallas_call(functools.partial(kernel, count_x, count_y, slot), out_sha...  23.6 us
    unnamed x7, local copies, waits for them, and re-layouts  0.85 us
    add x1, other arithmetic, local(): return (read, velocity_next, grain_position + velocity_next)  0.61 us

profile of v4, /device:TPU:0, one launch (start us, length us, event | category | flops | bytes accessed | tf_op | source)
XLA Modules:
  0.0 25.7 jit_solution(9377926896525865815)
XLA Ops:
  0.6 23.6 %step.1 = (f32[19,8,8,128]{3,2,1,0:T(8,128)S(1)}, f32[3,512]{1,0:T(4,128)S(1)}) custom-call(f32[19,8,8,128]{3,2,1,0:T(8,128)} %pops_in.1, s32[8,8,128]{2,1,0:T(8,128)} %cells_in.1, s32[8,1,128]{2,1,0:T(1,128)} %bitcast.2, s32[2,1024]{1,0:T(2,128)} %pairs_in.1, f32[3,512]{1,0:T(4,128)} %position_in.1, f32[3,512]{1,0:T(4,128)} %velocity_in.1, f32[1,512]{1,0:T(1,128)} %bitcast.3), custom_call_target="tpu_custom_call" | custom-call | tf_op jit(solution)/shard_map/step/pallas_call | solution.py:532
  24.2 0.0 copy-start
  24.2 0.0 copy-start.1
  24.2 0.0 copy-start.2
  24.2 0.8 %copy.12 = f32[19,8,8,128]{3,2,1,0:T(8,128)} copy(f32[19,8,8,128]{3,2,1,0:T(8,128)S(1)} %get-tuple-element.9) | data formatting | bytes 1245184
  25.1 0.0 copy-done
  25.1 0.0 copy-done.1
  25.1 0.0 copy-done.2
  25.1 0.6 %fusion = (f32[3,512]{1,0:T(4,128)}, f32[3,512]{1,0:T(4,128)}) fusion(f32[3,512]{1,0:T(4,128)S(1)} %copy-done, f32[3,512]{1,0:T(4,128)S(1)} %copy-done.1, f32[3,512]{1,0:T(4,128)S(1)} %get-tuple-element.6, f32[512]{0:T(512)S(1)} %copy-done.2), kind=kLoop, calls=%fused_computation.1 | loop fusion | flops 4608 | bytes 32768 | tf_op jit(solution)/shard_map/add | solution.py:588
Async XLA Ops:
  24.2 0.9 %copy-start = (f32[3,512]{1,0:T(4,128)S(1)}, f32[3,512]{1,0:T(4,128)}, u32[]{:S(2)}) copy-start(f32[3,512]{1,0:T(4,128)} %position_in.1) | copy-start | bytes 18436
  24.2 0.9 %copy-start.1 = (f32[3,512]{1,0:T(4,128)S(1)}, f32[3,512]{1,0:T(4,128)}, u32[]{:S(2)}) copy-start(f32[3,512]{1,0:T(4,128)} %velocity_in.1) | copy-start | bytes 18436
  24.2 0.8 %copy-start.2 = (f32[512]{0:T(512)S(1)}, f32[512]{0:T(512)}, u32[]{:S(2)}) copy-start(f32[512]{0:T(512)} %param.15) | copy-start | bytes 6148
